TPU v7x, 256 devices: a whole 4x4x8 slice. The times are simulated.
256 devices in a mesh: tm: 8 (over x_lo, y), space: 32 (over x_hi, z, core).
Axes of the slice: x: 4 (x_hi: 2, x_lo: 2; x = x_hi * 2 + x_lo), y: 4, z: 8, core: 2. Of those that a mesh axis runs over, the one named last changes fastest.
Arguments:
- initial_state: float32 [64, 256, 256], P('space'), may hold values from -6 to 6
- capacity: float32 [64, 256, 256], P('space'), may hold values from 0.5 to 2
- source: float32 [64, 256, 256], P('space'), may hold values from -6 to 6
- control: float32 [8, 16], P('tm'), may hold values from -2 to 2
- segment_index: int32 [64, 256], P('space'), may hold values from 0 to 15
Outputs:
- slice_ends: float32 [8, 64, 256, 256], P('tm', 'space')
All inputs are finite; a program needn't handle non-finite values.
Results may differ from a plain program's by a relative error of at most 0.0001.
Values sent between devices are 32-bit elements; how exact they have to be, the bound alone decides.
No kernel may reach another device: no remote copies, remote signals or barrier semaphores. Data moves between devices by JAX's collectives and lax.ppermute only.
A program may use at most 64 MiB of HBM per device.

v0:
```python
import jax
import jax.numpy as jnp
from jax import lax
from jax.sharding import PartitionSpec as P

SWEEPS = 6
CORRECTIONS = 2


step_fine = 1.0
step_coarse = 0.08


def extended_2(block, sides, width):
    for axis, dim in sides:
        count = lax.axis_size(axis)
        forward = [(i, i + 1) for i in range(count - 1)]
        backward = [(target, source) for source, target in forward]
        low = lax.ppermute(
            lax.slice_in_dim(block, block.shape[dim] - width, None, axis=dim), axis, forward
        )
        high = lax.ppermute(lax.slice_in_dim(block, 0, width, axis=dim), axis, backward)
        block = jnp.concatenate([low, block, high], axis=dim)
    return block


def laid_out(pieces, dim):
    shape = list(pieces.shape[1:])
    shape[dim] *= pieces.shape[0]
    return jnp.moveaxis(pieces, 0, dim).reshape(shape)


def from_everyone(array, axis):
    copies = jnp.broadcast_to(array, (lax.axis_size(axis), *array.shape))
    return lax.all_to_all(copies, axis, split_axis=0, concat_axis=0, tiled=True)


def gathered_copies(array, axis, dim):
    return laid_out(from_everyone(array, axis), dim)


def neighbours(extended):
    core = extended[1:-1]
    total = extended[2:] + extended[:-2]
    wide = jnp.pad(core, ((0, 0), (1, 1), (0, 0)))
    total = total + wide[:, 2:] + wide[:, :-2]
    deeper = jnp.pad(core, ((0, 0), (0, 0), (1, 1)))
    return total + deeper[:, :, 2:] + deeper[:, :, :-2]


def jacobi_sweep(extended, previous, capacity, forcing, divisor):
    return (capacity * previous + step_fine * forcing + step_fine * neighbours(extended)) / divisor


def coarse_value_of(state, scale, forcing):
    extended = extended_2(state, (("space", 0),), 1)
    core = extended[1:-1]
    return core + scale * (neighbours(extended) - 6.0 * core + forcing)


def forcing_from(source, segment_index, control_row):
    matches = segment_index[:, None, :] == lax.broadcasted_iota(
        jnp.int32, (1, control_row.shape[0], 1), 1
    )
    values = jnp.sum(
        jnp.where(matches, control_row[None, :, None], jnp.zeros((), jnp.float32)), axis=1
    )
    return source + jnp.pad(values[:, None, :], ((0, 0), (0, source.shape[1] - 1), (0, 0)))


def on_device(initial_state, capacity, source, control, segment_index):
    planes = capacity.shape[0]
    forcing = forcing_from(source, segment_index, control[0])
    divisor = capacity + 6.0 * step_fine
    scale = step_coarse / capacity
    my_slice = lax.axis_index("tm")
    time_groups = lax.axis_size("tm")
    stacked = extended_2(jnp.stack([capacity, forcing]), (("space", 1),), 1)
    capacity_wide = stacked[0]
    forcing_wide = stacked[1]
    divisor_wide = capacity_wide + 6.0 * step_fine
    global_plane = lax.axis_index("space") * planes + jnp.arange(planes + 2, dtype=jnp.int32) - 1
    inside_grid = (global_plane >= 0) & (global_plane < planes * lax.axis_size("space"))
    all_rows = gathered_copies(control, "tm", 0)

    def run_chain(correction_term, first_chain):
        if first_chain:
            every_term = None
        else:
            every_term = lax.all_gather(correction_term[None], "tm", axis=0, tiled=True)

        def chain_section(section_index, state):
            row = lax.dynamic_index_in_dim(all_rows, section_index, 0, keepdims=False)
            section_forcing = forcing_from(source, segment_index, row)
            following = coarse_value_of(state, scale, section_forcing)
            if every_term is not None:
                following = following + lax.dynamic_index_in_dim(
                    every_term, section_index, 0, keepdims=False
                )
            return jnp.where(section_index < my_slice, following, state)

        start_state = lax.fori_loop(0, time_groups - 1, chain_section, initial_state)
        coarse_value = coarse_value_of(start_state, scale, forcing)
        return (start_state, coarse_value, coarse_value + correction_term)

    start_state, coarse_value, end_state = run_chain(jnp.zeros_like(initial_state), True)
    for correction_index in range(CORRECTIONS):
        fine_state = start_state
        iterate = fine_state
        for sweep_pair in range(SWEEPS // 2):
            extended = extended_2(iterate, (("space", 0),), 2)
            if sweep_pair == 0:
                state_wide = extended[1:-1]
            middle = jacobi_sweep(extended, state_wide, capacity_wide, forcing_wide, divisor_wide)
            middle = jnp.where(inside_grid[:, None, None], middle, jnp.zeros((), jnp.float32))
            iterate = jacobi_sweep(middle, fine_state, capacity, forcing, divisor)
        fine_state = iterate
        correction_term = fine_state - coarse_value
        start_state, coarse_value, end_state = run_chain(correction_term, False)
    return end_state[None]


def solution(mesh):
    in_specs = (
        P("space", None, None),
        P("space", None, None),
        P("space", None, None),
        P("tm", None),
        P("space", None),
    )
    out_specs = P("tm", "space", None, None)
    return jax.shard_map(
        on_device, mesh=mesh, in_specs=in_specs, out_specs=out_specs, check_vma=False
    )
```

profile of v0, /device:TPU:4, one launch (start us, length us, event | category | flops | bytes accessed | tf_op | source)
XLA Modules:
  0.0 685.8 jit_solution(8740545162507706784)
XLA Ops:
  27.7 110.3 %while.45 = (s32[]{:T(128)}, f32[2,256,256]{2,0,1:T(2,128)S(1)}, s32[]{:T(128)}, s32[2,256]{1,0:T(2,128)S(1)}, f32[8,16]{1,0:T(8,128)S(1)}, /*index=5*/f32[2,256...) while((s32[]{:T(128)}, f32[2,256,256]{2,0,1:T(2,128)S(1)}, s32[]{:T(128)}, s32[2,256]{1,0:T(2,128)S(1)}, ...), condition=%wide.region_2.3_spmd, body=%wide.region_0.0_spmd.sunk | while | flops 1859075 | bytes 6822267 | solution.py:102
  45.9 7.4 %collective-permute-start.1 = (f32[1,256,256]{2,0,1:T(1,128)S(1)}, f32[1,256,256]{2,0,1:T(1,128)S(1)}, u32[]{:S(2)}, u32[]{:S(2)}) collective-permute-start(f32[1,256,256]{2,0,1:T(1,128)S(1)} %get-tuple-element.805), channel_id=1, source_target_pairs={{1,0},{2,1},{3,2},{4,3},{5,4},{6,5},{7,6},{8,7},{9,8},{10,9},{11,1... | collective-permute-start | bytes 786440 | tf_op jit(solution)/shard_map/while/body/eval_jaxpr/ppermute | solution.py:22
  61.6 7.4 %collective-permute-start.1 = (f32[1,256,256]{2,0,1:T(1,128)S(1)}, f32[1,256,256]{2,0,1:T(1,128)S(1)}, u32[]{:S(2)}, u32[]{:S(2)}) collective-permute-start(f32[1,256,256]{2,0,1:T(1,128)S(1)} %get-tuple-element.805), channel_id=1, source_target_pairs={{1,0},{2,1},{3,2},{4,3},{5,4},{6,5},{7,6},{8,7},{9,8},{10,9},{11,1... | collective-permute-start | bytes 786440 | tf_op jit(solution)/shard_map/while/body/eval_jaxpr/ppermute | solution.py:22
  77.4 7.4 %collective-permute-start.1 = (f32[1,256,256]{2,0,1:T(1,128)S(1)}, f32[1,256,256]{2,0,1:T(1,128)S(1)}, u32[]{:S(2)}, u32[]{:S(2)}) collective-permute-start(f32[1,256,256]{2,0,1:T(1,128)S(1)} %get-tuple-element.805), channel_id=1, source_target_pairs={{1,0},{2,1},{3,2},{4,3},{5,4},{6,5},{7,6},{8,7},{9,8},{10,9},{11,1... | collective-permute-start | bytes 786440 | tf_op jit(solution)/shard_map/while/body/eval_jaxpr/ppermute | solution.py:22
  93.2 7.4 %collective-permute-start.1 = (f32[1,256,256]{2,0,1:T(1,128)S(1)}, f32[1,256,256]{2,0,1:T(1,128)S(1)}, u32[]{:S(2)}, u32[]{:S(2)}) collective-permute-start(f32[1,256,256]{2,0,1:T(1,128)S(1)} %get-tuple-element.805), channel_id=1, source_target_pairs={{1,0},{2,1},{3,2},{4,3},{5,4},{6,5},{7,6},{8,7},{9,8},{10,9},{11,1... | collective-permute-start | bytes 786440 | tf_op jit(solution)/shard_map/while/body/eval_jaxpr/ppermute | solution.py:22
  109.0 7.4 %collective-permute-start.1 = (f32[1,256,256]{2,0,1:T(1,128)S(1)}, f32[1,256,256]{2,0,1:T(1,128)S(1)}, u32[]{:S(2)}, u32[]{:S(2)}) collective-permute-start(f32[1,256,256]{2,0,1:T(1,128)S(1)} %get-tuple-element.805), channel_id=1, source_target_pairs={{1,0},{2,1},{3,2},{4,3},{5,4},{6,5},{7,6},{8,7},{9,8},{10,9},{11,1... | collective-permute-start | bytes 786440 | tf_op jit(solution)/shard_map/while/body/eval_jaxpr/ppermute | solution.py:22
  124.8 7.4 %collective-permute-start.1 = (f32[1,256,256]{2,0,1:T(1,128)S(1)}, f32[1,256,256]{2,0,1:T(1,128)S(1)}, u32[]{:S(2)}, u32[]{:S(2)}) collective-permute-start(f32[1,256,256]{2,0,1:T(1,128)S(1)} %get-tuple-element.805), channel_id=1, source_target_pairs={{1,0},{2,1},{3,2},{4,3},{5,4},{6,5},{7,6},{8,7},{9,8},{10,9},{11,1... | collective-permute-start | bytes 786440 | tf_op jit(solution)/shard_map/while/body/eval_jaxpr/ppermute | solution.py:22
  138.0 7.4 %collective-permute-start.9 = (f32[2,256,256]{2,0,1:T(2,128)S(1)}, f32[2,256,256]{2,0,1:T(2,128)S(1)}, u32[]{:S(2)}, u32[]{:S(2)}) collective-permute-start(f32[2,256,256]{2,0,1:T(2,128)S(1)} %get-tuple-element.577), channel_id=1, source_target_pairs={{1,0},{2,1},{3,2},{4,3},{5,4},{6,5},{7,6},{8,7},{9,8},{10,9},{11,1... | collective-permute-start | bytes 1572872 | tf_op jit(solution)/shard_map/ppermute | solution.py:22
  152.2 7.4 %collective-permute-done.8 = f32[2,256,256]{2,0,1:T(2,128)S(1)} collective-permute-done((f32[2,256,256]{2,0,1:T(2,128)S(1)}, f32[2,256,256]{2,0,1:T(2,128)S(1)}, u32[]{:S(2)}, u32[]{:S(2)}) %collective-permute-start.8) | collective-permute-done | bytes 524320 | tf_op jit(solution)/shard_map/ppermute | solution.py:19
  169.3 7.4 %collective-permute-start.10 = (f32[2,256,256]{2,0,1:T(2,128)S(1)}, f32[2,256,256]{2,0,1:T(2,128)S(1)}, u32[]{:S(2)}, u32[]{:S(2)}) collective-permute-start(f32[2,256,256]{2,0,1:T(2,128)S(1)} %fusion.73), channel_id=1, source_target_pairs={{1,0},{2,1},{3,2},{4,3},{5,4},{6,5},{7,6},{8,7},{9,8},{10,9},{11,1... | collective-permute-start | bytes 1572872 | tf_op jit(solution)/shard_map/ppermute | solution.py:22
  190.9 7.4 %collective-permute-start.12 = (f32[2,256,256]{2,0,1:T(2,128)S(1)}, f32[2,256,256]{2,0,1:T(2,128)S(1)}, u32[]{:S(2)}, u32[]{:S(2)}) collective-permute-start(f32[2,256,256]{2,0,1:T(2,128)S(1)} %fusion.77), channel_id=1, source_target_pairs={{1,0},{2,1},{3,2},{4,3},{5,4},{6,5},{7,6},{8,7},{9,8},{10,9},{11,1... | collective-permute-start | bytes 1572872 | tf_op jit(solution)/shard_map/ppermute | solution.py:22
  217.2 51.6 %all-gather.5.cloned.1.call-done = f32[16,256,256]{2,1,0:T(8,128)} async-done(((f32[2,256,256]{2,1,0:T(8,128)}), f32[16,256,256]{2,1,0:T(8,128)}) %all-gather.5.cloned.1.call-update) | async-done | bytes 4194320 | tf_op jit(solution)/shard_map/all_gather | solution.py:90
  268.7 129.7 %while.46 = (s32[]{:T(128)}, f32[2,256,256]{2,0,1:T(2,128)S(1)}, s32[]{:T(128)}, s32[2,256]{1,0:T(2,128)S(1)}, f32[8,16]{1,0:T(8,128)S(1)}, /*index=5*/f32[2,256...) while((s32[]{:T(128)}, f32[2,256,256]{2,0,1:T(2,128)S(1)}, ...), condition=%wide.region_6.7_spmd, body=%wide.region_4.6_spmd.sunk | while | flops 1990147 | bytes 9443747 | solution.py:102
  290.3 7.4 %collective-permute-start.3 = (f32[1,256,256]{2,0,1:T(1,128)S(1)}, f32[1,256,256]{2,0,1:T(1,128)S(1)}, u32[]{:S(2)}, u32[]{:S(2)}) collective-permute-start(f32[1,256,256]{2,0,1:T(1,128)S(1)} %get-tuple-element.815), channel_id=1, source_target_pairs={{1,0},{2,1},{3,2},{4,3},{5,4},{6,5},{7,6},{8,7},{9,8},{10,9},{11,1... | collective-permute-start | bytes 786440 | tf_op jit(solution)/shard_map/while/body/eval_jaxpr/ppermute | solution.py:22
  308.9 7.4 %collective-permute-start.3 = (f32[1,256,256]{2,0,1:T(1,128)S(1)}, f32[1,256,256]{2,0,1:T(1,128)S(1)}, u32[]{:S(2)}, u32[]{:S(2)}) collective-permute-start(f32[1,256,256]{2,0,1:T(1,128)S(1)} %get-tuple-element.815), channel_id=1, source_target_pairs={{1,0},{2,1},{3,2},{4,3},{5,4},{6,5},{7,6},{8,7},{9,8},{10,9},{11,1... | collective-permute-start | bytes 786440 | tf_op jit(solution)/shard_map/while/body/eval_jaxpr/ppermute | solution.py:22
  398.5 7.6 %collective-permute-start.17 = (f32[2,256,256]{2,0,1:T(2,128)S(1)}, f32[2,256,256]{2,0,1:T(2,128)S(1)}, u32[]{:S(2)}, u32[]{:S(2)}) collective-permute-start(f32[2,256,256]{2,0,1:T(2,128)S(1)} %get-tuple-element.578), channel_id=1, source_target_pairs={{1,0},{2,1},{3,2},{4,3},{5,4},{6,5},{7,6},{8,7},{9,8},{10,9},{11,1... | collective-permute-start | bytes 1572872 | tf_op jit(solution)/shard_map/ppermute | solution.py:22
  412.7 7.4 %collective-permute-done.16 = f32[2,256,256]{2,0,1:T(2,128)S(1)} collective-permute-done((f32[2,256,256]{2,0,1:T(2,128)S(1)}, f32[2,256,256]{2,0,1:T(2,128)S(1)}, u32[]{:S(2)}, u32[]{:S(2)}) %collective-permute-start.16) | collective-permute-done | bytes 524320 | tf_op jit(solution)/shard_map/ppermute | solution.py:19
  449.7 7.4 %collective-permute-start.20 = (f32[2,256,256]{2,0,1:T(2,128)S(1)}, f32[2,256,256]{2,0,1:T(2,128)S(1)}, u32[]{:S(2)}, u32[]{:S(2)}) collective-permute-start(f32[2,256,256]{2,0,1:T(2,128)S(1)} %fusion.93), channel_id=1, source_target_pairs={{1,0},{2,1},{3,2},{4,3},{5,4},{6,5},{7,6},{8,7},{9,8},{10,9},{11,1... | collective-permute-start | bytes 1572872 | tf_op jit(solution)/shard_map/ppermute | solution.py:22
  476.5 48.9 %all-gather.7.cloned.1.call-done = f32[16,256,256]{2,1,0:T(8,128)} async-done(((f32[2,256,256]{2,1,0:T(8,128)}), f32[16,256,256]{2,1,0:T(8,128)}) %all-gather.7.cloned.1.call-update) | async-done | bytes 4194320 | tf_op jit(solution)/shard_map/all_gather | solution.py:90
  525.5 129.8 %while.47 = (s32[]{:T(128)}, f32[2,256,256]{2,0,1:T(2,128)S(1)}, s32[]{:T(128)}, s32[2,256]{1,0:T(2,128)S(1)}, f32[8,16]{1,0:T(8,128)S(1)}, /*index=5*/f32[2,256...) while((s32[]{:T(128)}, f32[2,256,256]{2,0,1:T(2,128)S(1)}, ...), condition=%wide.region_9.10_spmd, body=%wide.region_7.9_spmd.sunk | while | flops 1990147 | bytes 9443747 | solution.py:102
  565.6 7.4 %collective-permute-start.5 = (f32[1,256,256]{2,0,1:T(1,128)S(1)}, f32[1,256,256]{2,0,1:T(1,128)S(1)}, u32[]{:S(2)}, u32[]{:S(2)}) collective-permute-start(f32[1,256,256]{2,0,1:T(1,128)S(1)} %get-tuple-element.825), channel_id=1, source_target_pairs={{1,0},{2,1},{3,2},{4,3},{5,4},{6,5},{7,6},{8,7},{9,8},{10,9},{11,1... | collective-permute-start | bytes 786440 | tf_op jit(solution)/shard_map/while/body/eval_jaxpr/ppermute | solution.py:22
  602.8 7.4 %collective-permute-start.5 = (f32[1,256,256]{2,0,1:T(1,128)S(1)}, f32[1,256,256]{2,0,1:T(1,128)S(1)}, u32[]{:S(2)}, u32[]{:S(2)}) collective-permute-start(f32[1,256,256]{2,0,1:T(1,128)S(1)} %get-tuple-element.825), channel_id=1, source_target_pairs={{1,0},{2,1},{3,2},{4,3},{5,4},{6,5},{7,6},{8,7},{9,8},{10,9},{11,1... | collective-permute-start | bytes 786440 | tf_op jit(solution)/shard_map/while/body/eval_jaxpr/ppermute | solution.py:22
  655.7 7.4 %collective-permute-start.24 = (f32[1,256,256]{2,0,1:T(1,128)S(1)}, f32[1,256,256]{2,0,1:T(1,128)S(1)}, u32[]{:S(2)}, u32[]{:S(2)}) collective-permute-start(f32[1,256,256]{2,0,1:T(1,128)S(1)} %get-tuple-element.661), channel_id=1, source_target_pairs={{1,0},{2,1},{3,2},{4,3},{5,4},{6,5},{7,6},{8,7},{9,8},{10,9},{11,1... | collective-permute-start | bytes 786440 | tf_op jit(solution)/shard_map/ppermute | solution.py:22
  667.0 7.4 %collective-permute-done.25 = f32[1,256,256]{2,0,1:T(1,128)S(1)} collective-permute-done((f32[1,256,256]{2,0,1:T(1,128)S(1)}, f32[1,256,256]{2,0,1:T(1,128)S(1)}, u32[]{:S(2)}, u32[]{:S(2)}) %collective-permute-start.25) | collective-permute-done | bytes 262176 | tf_op jit(solution)/shard_map/ppermute | solution.py:19
  (320 shorter events, 428.5 us)
Async XLA Ops:
  7.8 19.9 %all-to-all-start = ((f32[8,1,16]{2,1,0:T(1,128)}), f32[8,1,16]{2,1,0:T(1,128)S(1)}, u32[]{:S(2)}, u32[]{:S(2)}) async-start(f32[8,1,16]{2,1,0:T(1,128)} %broadcast_in_dim.213), calls=%async_computation | async-start | bytes 8192 | tf_op jit(solution)/shard_map/all_to_all | solution.py:35
  12.9 255.9 %all-gather.5.cloned.1.call-start = ((), (), s32[]{:S(2)}) async-start(), calls=%async_computation.1 | async-start | bytes 4718592 | tf_op jit(solution)/shard_map/all_gather | solution.py:90
  17.9 129.6 %collective-permute-start.6 = (f32[2,1,256,256]{3,1,2,0:T(1,128)}, f32[2,1,256,256]{3,1,2,0:T(1,128)}, u32[]{:S(2)}, u32[]{:S(2)}) collective-permute-start(f32[2,1,256,256]{3,1,2,0:T(1,128)} %get-tuple-element.659), channel_id=1, source_target_pairs={{0,1},{1,2},{2,3},{3,4},{4,5},{5,6},{6,7},{7,8},{8,9},{9,10},{10,1... | collective-permute-start | bytes 1572872 | tf_op jit(solution)/shard_map/ppermute | solution.py:19
  19.8 127.7 %collective-permute-start.7 = (f32[2,1,256,256]{3,1,2,0:T(1,128)}, f32[2,1,256,256]{3,1,2,0:T(1,128)}, u32[]{:S(2)}, u32[]{:S(2)}) collective-permute-start(f32[2,1,256,256]{3,1,2,0:T(1,128)} %get-tuple-element.660), channel_id=1, source_target_pairs={{1,0},{2,1},{3,2},{4,3},{5,4},{6,5},{7,6},{8,7},{9,8},{10,9},{11,1... | collective-permute-start | bytes 1572872 | tf_op jit(solution)/shard_map/ppermute | solution.py:22
  138.0 14.1 %collective-permute-start.9 = (f32[2,256,256]{2,0,1:T(2,128)S(1)}, f32[2,256,256]{2,0,1:T(2,128)S(1)}, u32[]{:S(2)}, u32[]{:S(2)}) collective-permute-start(f32[2,256,256]{2,0,1:T(2,128)S(1)} %get-tuple-element.577), channel_id=1, source_target_pairs={{1,0},{2,1},{3,2},{4,3},{5,4},{6,5},{7,6},{8,7},{9,8},{10,9},{11,1... | collective-permute-start | bytes 1572872 | tf_op jit(solution)/shard_map/ppermute | solution.py:22
  145.5 14.1 %collective-permute-start.8 = (f32[2,256,256]{2,0,1:T(2,128)S(1)}, f32[2,256,256]{2,0,1:T(2,128)S(1)}, u32[]{:S(2)}, u32[]{:S(2)}) collective-permute-start(f32[2,256,256]{2,0,1:T(2,128)S(1)} %get-tuple-element.577), channel_id=1, source_target_pairs={{0,1},{1,2},{2,3},{3,4},{4,5},{5,6},{6,7},{7,8},{8,9},{9,10},{10,1... | collective-permute-start | bytes 1572872 | tf_op jit(solution)/shard_map/ppermute | solution.py:19
  167.3 14.1 %collective-permute-start.11 = (f32[2,256,256]{2,0,1:T(2,128)S(1)}, f32[2,256,256]{2,0,1:T(2,128)S(1)}, u32[]{:S(2)}, u32[]{:S(2)}) collective-permute-start(f32[2,256,256]{2,0,1:T(2,128)S(1)} %fusion.73), channel_id=1, source_target_pairs={{0,1},{1,2},{2,3},{3,4},{4,5},{5,6},{6,7},{7,8},{8,9},{9,10},{10,1... | collective-permute-start | bytes 1572872 | tf_op jit(solution)/shard_map/ppermute | solution.py:19
  169.3 13.9 %collective-permute-start.10 = (f32[2,256,256]{2,0,1:T(2,128)S(1)}, f32[2,256,256]{2,0,1:T(2,128)S(1)}, u32[]{:S(2)}, u32[]{:S(2)}) collective-permute-start(f32[2,256,256]{2,0,1:T(2,128)S(1)} %fusion.73), channel_id=1, source_target_pairs={{1,0},{2,1},{3,2},{4,3},{5,4},{6,5},{7,6},{8,7},{9,8},{10,9},{11,1... | collective-permute-start | bytes 1572872 | tf_op jit(solution)/shard_map/ppermute | solution.py:22
  189.0 14.3 %collective-permute-start.13 = (f32[2,256,256]{2,0,1:T(2,128)S(1)}, f32[2,256,256]{2,0,1:T(2,128)S(1)}, u32[]{:S(2)}, u32[]{:S(2)}) collective-permute-start(f32[2,256,256]{2,0,1:T(2,128)S(1)} %fusion.77), channel_id=1, source_target_pairs={{0,1},{1,2},{2,3},{3,4},{4,5},{5,6},{6,7},{7,8},{8,9},{9,10},{10,1... | collective-permute-start | bytes 1572872 | tf_op jit(solution)/shard_map/ppermute | solution.py:19
  190.9 14.1 %collective-permute-start.12 = (f32[2,256,256]{2,0,1:T(2,128)S(1)}, f32[2,256,256]{2,0,1:T(2,128)S(1)}, u32[]{:S(2)}, u32[]{:S(2)}) collective-permute-start(f32[2,256,256]{2,0,1:T(2,128)S(1)} %fusion.77), channel_id=1, source_target_pairs={{1,0},{2,1},{3,2},{4,3},{5,4},{6,5},{7,6},{8,7},{9,8},{10,9},{11,1... | collective-permute-start | bytes 1572872 | tf_op jit(solution)/shard_map/ppermute | solution.py:22
  216.9 308.5 %all-gather.7.cloned.1.call-start = ((), (), s32[]{:S(2)}) async-start(), calls=%async_computation.2 | async-start | bytes 4718592 | tf_op jit(solution)/shard_map/all_gather | solution.py:90
  325.5 11.7 %collective-permute-start.2 = (f32[1,256,256]{2,0,1:T(1,128)}, f32[1,256,256]{2,0,1:T(1,128)S(1)}, u32[]{:S(2)}, u32[]{:S(2)}) collective-permute-start(f32[1,256,256]{2,0,1:T(1,128)} %get-tuple-element.814), channel_id=1, source_target_pairs={{0,1},{1,2},{2,3},{3,4},{4,5},{5,6},{6,7},{7,8},{8,9},{9,10},{10,1... | collective-permute-start | bytes 786440 | tf_op jit(solution)/shard_map/while/body/eval_jaxpr/ppermute | solution.py:19
  344.1 11.7 %collective-permute-start.2 = (f32[1,256,256]{2,0,1:T(1,128)}, f32[1,256,256]{2,0,1:T(1,128)S(1)}, u32[]{:S(2)}, u32[]{:S(2)}) collective-permute-start(f32[1,256,256]{2,0,1:T(1,128)} %get-tuple-element.814), channel_id=1, source_target_pairs={{0,1},{1,2},{2,3},{3,4},{4,5},{5,6},{6,7},{7,8},{8,9},{9,10},{10,1... | collective-permute-start | bytes 786440 | tf_op jit(solution)/shard_map/while/body/eval_jaxpr/ppermute | solution.py:19
  362.7 11.7 %collective-permute-start.2 = (f32[1,256,256]{2,0,1:T(1,128)}, f32[1,256,256]{2,0,1:T(1,128)S(1)}, u32[]{:S(2)}, u32[]{:S(2)}) collective-permute-start(f32[1,256,256]{2,0,1:T(1,128)} %get-tuple-element.814), channel_id=1, source_target_pairs={{0,1},{1,2},{2,3},{3,4},{4,5},{5,6},{6,7},{7,8},{8,9},{9,10},{10,1... | collective-permute-start | bytes 786440 | tf_op jit(solution)/shard_map/while/body/eval_jaxpr/ppermute | solution.py:19
  381.2 11.7 %collective-permute-start.2 = (f32[1,256,256]{2,0,1:T(1,128)}, f32[1,256,256]{2,0,1:T(1,128)S(1)}, u32[]{:S(2)}, u32[]{:S(2)}) collective-permute-start(f32[1,256,256]{2,0,1:T(1,128)} %get-tuple-element.814), channel_id=1, source_target_pairs={{0,1},{1,2},{2,3},{3,4},{4,5},{5,6},{6,7},{7,8},{8,9},{9,10},{10,1... | collective-permute-start | bytes 786440 | tf_op jit(solution)/shard_map/while/body/eval_jaxpr/ppermute | solution.py:19
  398.5 14.2 %collective-permute-start.17 = (f32[2,256,256]{2,0,1:T(2,128)S(1)}, f32[2,256,256]{2,0,1:T(2,128)S(1)}, u32[]{:S(2)}, u32[]{:S(2)}) collective-permute-start(f32[2,256,256]{2,0,1:T(2,128)S(1)} %get-tuple-element.578), channel_id=1, source_target_pairs={{1,0},{2,1},{3,2},{4,3},{5,4},{6,5},{7,6},{8,7},{9,8},{10,9},{11,1... | collective-permute-start | bytes 1572872 | tf_op jit(solution)/shard_map/ppermute | solution.py:22
  406.0 14.1 %collective-permute-start.16 = (f32[2,256,256]{2,0,1:T(2,128)S(1)}, f32[2,256,256]{2,0,1:T(2,128)S(1)}, u32[]{:S(2)}, u32[]{:S(2)}) collective-permute-start(f32[2,256,256]{2,0,1:T(2,128)S(1)} %get-tuple-element.578), channel_id=1, source_target_pairs={{0,1},{1,2},{2,3},{3,4},{4,5},{5,6},{6,7},{7,8},{8,9},{9,10},{10,1... | collective-permute-start | bytes 1572872 | tf_op jit(solution)/shard_map/ppermute | solution.py:19
  426.1 14.1 %collective-permute-start.19 = (f32[2,256,256]{2,0,1:T(2,128)S(1)}, f32[2,256,256]{2,0,1:T(2,128)S(1)}, u32[]{:S(2)}, u32[]{:S(2)}) collective-permute-start(f32[2,256,256]{2,0,1:T(2,128)S(1)} %fusion.89), channel_id=1, source_target_pairs={{0,1},{1,2},{2,3},{3,4},{4,5},{5,6},{6,7},{7,8},{8,9},{9,10},{10,1... | collective-permute-start | bytes 1572872 | tf_op jit(solution)/shard_map/ppermute | solution.py:19
  428.1 13.9 %collective-permute-start.18 = (f32[2,256,256]{2,0,1:T(2,128)S(1)}, f32[2,256,256]{2,0,1:T(2,128)S(1)}, u32[]{:S(2)}, u32[]{:S(2)}) collective-permute-start(f32[2,256,256]{2,0,1:T(2,128)S(1)} %fusion.89), channel_id=1, source_target_pairs={{1,0},{2,1},{3,2},{4,3},{5,4},{6,5},{7,6},{8,7},{9,8},{10,9},{11,1... | collective-permute-start | bytes 1572872 | tf_op jit(solution)/shard_map/ppermute | solution.py:22
  447.8 14.4 %collective-permute-start.21 = (f32[2,256,256]{2,0,1:T(2,128)S(1)}, f32[2,256,256]{2,0,1:T(2,128)S(1)}, u32[]{:S(2)}, u32[]{:S(2)}) collective-permute-start(f32[2,256,256]{2,0,1:T(2,128)S(1)} %fusion.93), channel_id=1, source_target_pairs={{0,1},{1,2},{2,3},{3,4},{4,5},{5,6},{6,7},{7,8},{8,9},{9,10},{10,1... | collective-permute-start | bytes 1572872 | tf_op jit(solution)/shard_map/ppermute | solution.py:19
  449.7 14.1 %collective-permute-start.20 = (f32[2,256,256]{2,0,1:T(2,128)S(1)}, f32[2,256,256]{2,0,1:T(2,128)S(1)}, u32[]{:S(2)}, u32[]{:S(2)}) collective-permute-start(f32[2,256,256]{2,0,1:T(2,128)S(1)} %fusion.93), channel_id=1, source_target_pairs={{1,0},{2,1},{3,2},{4,3},{5,4},{6,5},{7,6},{8,7},{9,8},{10,9},{11,1... | collective-permute-start | bytes 1572872 | tf_op jit(solution)/shard_map/ppermute | solution.py:22
  545.2 11.7 %collective-permute-start.4 = (f32[1,256,256]{2,0,1:T(1,128)}, f32[1,256,256]{2,0,1:T(1,128)S(1)}, u32[]{:S(2)}, u32[]{:S(2)}) collective-permute-start(f32[1,256,256]{2,0,1:T(1,128)} %get-tuple-element.824), channel_id=1, source_target_pairs={{0,1},{1,2},{2,3},{3,4},{4,5},{5,6},{6,7},{7,8},{8,9},{9,10},{10,1... | collective-permute-start | bytes 786440 | tf_op jit(solution)/shard_map/while/body/eval_jaxpr/ppermute | solution.py:19
  582.3 11.7 %collective-permute-start.4 = (f32[1,256,256]{2,0,1:T(1,128)}, f32[1,256,256]{2,0,1:T(1,128)S(1)}, u32[]{:S(2)}, u32[]{:S(2)}) collective-permute-start(f32[1,256,256]{2,0,1:T(1,128)} %get-tuple-element.824), channel_id=1, source_target_pairs={{0,1},{1,2},{2,3},{3,4},{4,5},{5,6},{6,7},{7,8},{8,9},{9,10},{10,1... | collective-permute-start | bytes 786440 | tf_op jit(solution)/shard_map/while/body/eval_jaxpr/ppermute | solution.py:19
  619.4 11.7 %collective-permute-start.4 = (f32[1,256,256]{2,0,1:T(1,128)}, f32[1,256,256]{2,0,1:T(1,128)S(1)}, u32[]{:S(2)}, u32[]{:S(2)}) collective-permute-start(f32[1,256,256]{2,0,1:T(1,128)} %get-tuple-element.824), channel_id=1, source_target_pairs={{0,1},{1,2},{2,3},{3,4},{4,5},{5,6},{6,7},{7,8},{8,9},{9,10},{10,1... | collective-permute-start | bytes 786440 | tf_op jit(solution)/shard_map/while/body/eval_jaxpr/ppermute | solution.py:19
  (66 other events, 608.1 us)
Sparse Core Ops, SparseCore 0:
  217.0 51.6 all-gather.4
  476.6 48.7 all-gather.6
where the time goes:
time: 689 us; the launch traced here: 686 us
  starting transfers between devices  285 us (41%)
  waiting for transfers between devices  221 us (32%)
  other arithmetic  109 us (16%)
  local copies, waits for them, and re-layouts  56.3 us (8%)
  between operations  14 us (2%)
    ppermute x31, starting transfers between devices, extended_2(): lax.ppermute(lax.slice_in_dim(block, 0, width, axis=dim), axis, backward)  220 us
    all_gather x2, waiting for transfers between devices, run_chain(): every_term = lax.all_gather(correction_term[None], 'tm', axis=0, tiled=True)  101 us
    ppermute x31, waiting for transfers between devices, extended_2(): lax.ppermute(lax.slice_in_dim(block, block.shape[dim] - width, None, axis...  70.9 us
    select_n x21, other arithmetic, chain_section(): return jnp.where(section_index < my_slice, following, state)  59.9 us
    ppermute x31, starting transfers between devices, extended_2(): lax.ppermute(lax.slice_in_dim(block, block.shape[dim] - width, None, axis...  59.8 us
    ppermute x31, waiting for transfers between devices, extended_2(): lax.ppermute(lax.slice_in_dim(block, 0, width, axis=dim), axis, backward)  49.1 us
    slice x24, local copies, waits for them, and re-layouts, extended_2(): lax.slice_in_dim(block, 0, width, axis=dim)  19.6 us
    dynamic_slice x14, local copies, waits for them, and re-layouts, chain_section(): lax.dynamic_index_in_dim(every_term, section_index, 0, keepdims=False)  15.1 us
  transfers between devices with their start and end apart: 65, of which 59 were waited for; matrix products, arithmetic and copies ran while one was open for 7% of the time, Pallas kernels for 0%

commit v1 on v0

v1 whole, which is shorter than its diff:
```python
import jax
import jax.numpy as jnp
import numpy as np
from jax import lax
from jax.experimental import pallas as pl
from jax.experimental.pallas import tpu as pltpu
from jax.sharding import Mesh
from jax.sharding import PartitionSpec as P

SWEEPS = 6
SLICES = 8
SEGMENTS = 16
COARSE = 0.08
AXES = ("tm", "chip", "core")
CHIPS = 16
PLANES = 38
ROWS = 72
OWN = 24
LANES = 128
REACH = 17


def device_pairs(target):
    pairs = []
    for t in range(8):
        for chip in range(CHIPS):
            for core in range(2):
                to = target(chip, core)
                if to is None or not 0 <= to[0] < CHIPS:
                    continue
                t_to = t if chip // 8 == to[0] // 8 else t ^ 4
                pairs.append(((t * CHIPS + chip) * 2 + core, (t_to * CHIPS + to[0]) * 2 + to[1]))
    return pairs


PARTNER = device_pairs(lambda chip, core: (chip, 1 - core))
OUTWARD = device_pairs(lambda chip, core: (chip + 1 - 2 * core, core))
OUTWARD_5 = device_pairs(lambda chip, core: (chip + 5 - 10 * core, core))
FACING = device_pairs(lambda chip, core: (chip - 1 + 2 * core, 1 - core))
FACING_SAME = device_pairs(lambda chip, core: (chip - 1 + 2 * core, core))


def send(x, pairs):
    return lax.ppermute(x, AXES, pairs)


def lane_order():
    order = np.zeros((256, 256), np.float32)
    for z in range(256):
        order[z, (z % 2) * LANES + z // 2] = 1.0
    return order


def tiles(r):
    out = {}
    for i in range(r + 2):
        rho = -(-(r - max(0, i - 1)) // 4)
        for k in range(2 + rho):
            out.setdefault(OWN - 4 * rho + 8 * k, []).append(i)
    return sorted(out.items())


def main_kernel(meta, steps, own_c, own_q, near_c, near_q, far_c, far_q, end_cq, pnear_c, pnear_q, pfar_c, pfar_q,
                pend_cq, order, out, sig, rd, q, va, vb, wa, wb, ua, ub, e, le, ha, hb, total, jumps, segs, ends, sems):
    core = meta[0]
    zero = meta[1]

    copies = []

    def copy(src, dst):
        c = pltpu.make_async_copy(src, dst, sems.at[len(copies)])
        c.start()
        copies.append(c)

    half = pl.multiple_of(core * 16, 8)
    for own, near, far, end, pnear, pfar, pend, dst in (
        (own_c, near_c, far_c, 0, pnear_c, pfar_c, 0, sig),
        (own_q, near_q, far_q, 1, pnear_q, pfar_q, 1, q),
    ):
        copy(own.at[:, :, pl.ds(half, 64), :], dst.at[pl.ds(REACH, 4), :, pl.ds(0, 64), :])
        for block, blocks, end_block, mine in ((near, far, end_cq, True), (pnear, pfar, pend_cq, False)):
            side = core if mine else 1 - core
            for k in range(1, 5):
                p = REACH - 4 * k + side * (8 * k)
                if k <= 2:
                    b = block.at[k - 1]
                    copy(b.at[:, :, pl.ds(half, 48), :], dst.at[pl.ds(p, 4), :, pl.ds(OWN - 16, 48), :])
                    if k == 1 and dst is q:
                        copy(b.at[:, :, pl.ds(8, 8), :], dst.at[pl.ds(p, 4), :, pl.ds(0, 8), :])
                else:
                    b = blocks.at[k - 3]
                    copy(b.at[:, :, pl.ds(half, 32), :], dst.at[pl.ds(p, 4), :, pl.ds(OWN - 8, 32), :])
            copy(end_block.at[end, :, pl.ds(half, 32), :],
                 dst.at[(PLANES - 1) * side, :, pl.ds(OWN - 8, 32), :])
    for c in copies:
        c.wait()

    lane = lax.broadcasted_iota(jnp.int32, (8, LANES), 1)
    row = lax.broadcasted_iota(jnp.int32, (8, LANES), 0)
    first, last = lane == 0, lane == LANES - 1

    def take_segments(p, _):
        for h in range(2):
            segs[h, pl.ds(p, 1), :] = q[p, h, pl.ds(16 * (1 - core), 1), :]
        return 0

    lax.fori_loop(0, PLANES, take_segments, 0)
    for h in range(2):
        s = segs[h]
        acc = [jnp.zeros_like(s) for _ in range(SLICES)]
        for m in range(SEGMENTS):
            hit = s == jnp.float32(m)
            acc = [jnp.where(hit, steps[n, m], a) for n, a in enumerate(acc)]
        for n in range(SLICES):
            jumps[0, n, h] = acc[n] * steps[SLICES, 0]
            if n < 2:
                jumps[1, n, h] = acc[n] * steps[SLICES, 1]

    def on_sides(*stages):
        def body(side, _):
            plane = [18 + side + (2 * side - 1) * i for i in range(-1, REACH + 2)]
            stores = []
            for stage in stages:
                stage(lambda i: plane[i + 1], stores)
            for ref, p, h, y, value in stores:
                ref[p, h, pl.ds(y, 8), :] = value
            return 0

        lax.fori_loop(0, 2, body, 0)

    def loader(plane):
        cache = {}

        def load(ref, i, h, y):
            key = (id(ref), i, h, y)
            if key not in cache:
                cache[key] = ref[plane(i), h, pl.ds(zero + y, 8), :]
            return cache[key]

        return load

    def around(ref, plane, load, i, y):
        even, odd = load(ref, i, 0, y), load(ref, i, 1, y)
        z = (odd + jnp.where(first, 0.0, pltpu.roll(odd, 1, 1)), even + jnp.where(last, 0.0, pltpu.roll(even, LANES - 1, 1)))
        sums = []
        for h in range(2):
            sums.append(z[h] + (load(ref, i, h, y - 1) + load(ref, i, h, y + 1))
                        + (load(ref, i - 1, h, y) + load(ref, i + 1, h, y)))
        return sums

    def jump(plane, n, i, h, y):
        result = None
        for which, at in ((0, OWN), (1, OWN - 16)):
            if y <= at < y + 8 and (which == 0 or n < 2):
                value = jnp.where(row == at - y, jumps[which, n, h, pl.ds(plane(i), 1), :], 0.0)
                result = value if result is None else result + value
        return result

    def setup(plane, stores):
        load = loader(plane)
        for y, planes in tiles(17):
            for i in planes:
                for h in range(2):
                    c = load(sig, i, h, y)
                    inside = c > 0.0
                    c = jnp.where(inside, c, 1.0)
                    s = jnp.where(inside, COARSE / c, 0.0)
                    d = jnp.where(inside, 1.0 / (c + 6.0), 0.0)
                    value = load(q, i, h, y)
                    change = jump(plane, 0, i, h, y)
                    p = plane(i)
                    if change is not None:
                        value = value + change
                        stores.append((q, p, h, zero + y, value))
                    stores += [(sig, p, h, zero + y, s), (rd, p, h, zero + y, d), (va, p, h, zero + y, s * value),
                               (wa, p, h, zero + y, d * value)]

    def advance(n, r, v_old, v_new):
        def stage(plane, stores):
            load = loader(plane)
            for y, planes in tiles(r):
                for i in planes:
                    sums = around(v_old, plane, load, i, y)
                    for h in range(2):
                        value = load(q, i, h, y) + (sums[h] - 6.0 * load(v_old, i, h, y))
                        change = jump(plane, n, i, h, y)
                        if change is not None:
                            value = value + change
                        p = plane(i)
                        stores.append((q, p, h, zero + y, value))
                        if n < SLICES - 1:
                            stores += [(v_new, p, h, zero + y, load(sig, i, h, y) * value),
                                       (wa, p, h, zero + y, load(rd, i, h, y) * value)]
        return stage

    def second_order(n, r):
        def stage(plane, stores):
            load = loader(plane)
            for y, planes in tiles(r):
                for i in planes:
                    sums = around(e, plane, load, i, y)
                    for h in range(2):
                        value = sums[h] - 6.0 * load(e, i, h, y)
                        p = plane(i)
                        stores += [(le, p, h, zero + y, value), (ua, p, h, zero + y, load(rd, i, h, y) * value)]
        return stage

    def with_source(plane, stores):
        load = loader(plane)
        for y, planes in tiles(5):
            for i in planes:
                for h in range(2):
                    value = load(le, i, h, y) + load(q, i, h, y)
                    p = plane(i)
                    stores += [(le, p, h, zero + y, value), (ua, p, h, zero + y, load(rd, i, h, y) * value)]

    def sweep(r, src, dst, source):
        def stage(plane, stores):
            load = loader(plane)
            for y, planes in tiles(r):
                for i in planes:
                    sums = around(src, plane, load, i, y)
                    for h in range(2):
                        stores.append((dst, plane(i), h, zero + y, load(rd, i, h, y) * (load(source, i, h, y) + sums[h])))
        return stage

    def finish_first(n, r, src):
        def stage(plane, stores):
            load = loader(plane)
            for y, planes in tiles(r):
                for i in planes:
                    sums = around(src, plane, load, i, y)
                    for h in range(2):
                        value = load(rd, i, h, y) * (load(q, i, h, y) + sums[h])
                        s = load(sig, i, h, y)
                        if n == 0:
                            value = value - s * load(q, i, h, y)
                        else:
                            value = load(e, i, h, y) + (value + s * (load(le, i, h, y) - load(q, i, h, y)))
                        stores.append((e, plane(i), h, zero + y, value))
        return stage

    def finish_second(n, r, src, h_old, h_new):
        def stage(plane, stores):
            load = loader(plane)
            for y, planes in tiles(r):
                for i in planes:
                    sums = around(src, plane, load, i, y)
                    around_h = around(h_old, plane, load, i, y) if n > 1 else None
                    for h in range(2):
                        value = load(rd, i, h, y) * (load(le, i, h, y) + sums[h])
                        s = load(sig, i, h, y)
                        coarse = None
                        if n > 1:
                            coarse = around_h[h] - 6.0 * load(h_old, i, h, y)
                        if n < SLICES - 1:
                            own = load(le, i, h, y)
                            coarse = -own if coarse is None else coarse - own
                        value = value + s * coarse
                        if n > 1:
                            value = load(h_old, i, h, y) + value
                        if n < SLICES - 1:
                            stores.append((h_new, plane(i), h, zero + y, value))
                        else:
                            emit(plane, stores, n, i, h, y, load(total, plane(i) - REACH - i + i, h, y) if False else None, value)
        return stage

    def emit(plane, stores, n, i, h, y, _, value):
        p = plane(i) - REACH
        value = value + total[p, h, pl.ds(y - OWN, 8), :] + e[plane(i), h, pl.ds(y, 8), :]
        stores.append((ends, n * 4 + p, h, y - OWN, value))

    def close(n, v):
        def stage(plane, stores):
            for y, planes in tiles(0):
                for i in planes:
                    for h in range(2):
                        p = plane(i) - REACH
                        value = v[plane(i), h, pl.ds(y, 8), :]
                        if n > 0:
                            value = value + total[p, h, pl.ds(y - OWN, 8), :]
                        stores.append((total, p, h, y - OWN, value))
                        value = value + e[plane(i), h, pl.ds(y, 8), :]
                        if n > 0:
                            h_now = ha if n % 2 == 0 else hb
                            value = value + h_now[plane(i), h, pl.ds(y, 8), :]
                        stores.append((ends, n * 4 + p, h, y - OWN, value))
        return stage

    on_sides(setup)
    v_now, v_next = va, vb
    for n in range(SLICES):
        if n > 0:
            stages = [close(n - 1, v_now), second_order(n, min(12 - n, 12))]
            r = 17 - n if n < SLICES - 1 else 5
            stages.append(advance(n, r, v_now, v_next))
            on_sides(*stages)
            v_now, v_next = v_next, v_now
            if n == SLICES - 1:
                on_sides(with_source)
        w_src, w_dst, u_src, u_dst = wa, wb, ua, ub
        for k in range(2, SWEEPS + 1):
            stages = []
            if n < SLICES - 1:
                r = 18 - n - k
                stages.append(sweep(r, w_src, w_dst, q) if k < SWEEPS else finish_first(n, r, w_src))
            if n > 0:
                r = 13 - n - k
                if k < SWEEPS:
                    stages.append(sweep(r, u_src, u_dst, le))
                else:
                    h_old, h_new = (ha, hb) if n % 2 == 1 else (hb, ha)
                    stages.append(finish_second(n, r, u_src, h_old, h_new))
            on_sides(*stages)
            w_src, w_dst, u_src, u_dst = w_dst, w_src, u_dst, u_src

    for n in range(SLICES):
        for p in range(4):
            tile = ends[n * 4 + p]
            both = jnp.concatenate([tile[0], tile[1]], axis=1)
            out[n, p] = lax.dot_general(both, order[...], (((1,), (1,)), ((), ())), precision=lax.Precision.HIGHEST,
                                        preferred_element_type=jnp.float32)


def solve(meta, steps, *blocks):
    field = pltpu.VMEM((PLANES, 2, ROWS, LANES), jnp.float32)
    order = jnp.asarray(lane_order())
    any_space = pl.BlockSpec(memory_space=pl.ANY)
    smem = pl.BlockSpec(memory_space=pltpu.SMEM)
    vmem = pl.BlockSpec(memory_space=pltpu.VMEM)
    return pl.pallas_call(
        main_kernel,
        out_shape=jax.ShapeDtypeStruct((SLICES, 4, 16, 256), jnp.float32),
        in_specs=[smem, smem] + [any_space] * len(blocks) + [vmem],
        out_specs=vmem,
        scratch_shapes=[field] * 13 + [
            pltpu.VMEM((4, 2, 16, LANES), jnp.float32),
            pltpu.VMEM((2, SLICES, 2, 40, LANES), jnp.float32),
            pltpu.VMEM((2, 40, LANES), jnp.float32),
            pltpu.VMEM((SLICES * 4, 2, 16, LANES), jnp.float32),
            pltpu.SemaphoreType.DMA((32,)),
        ],
        compiler_params=pltpu.CompilerParams(vmem_limit_bytes=60 << 20),
        name="parareal",
    )(meta, steps, *blocks, order)


def on_device(initial_state, capacity, source, control, segment_index):
    tm, chip, core = lax.axis_index("tm"), lax.axis_index("chip"), lax.axis_index("core")
    block = jnp.where(chip >= CHIPS // 2, tm ^ 4, tm)
    controls = lax.all_gather(control, "tm", axis=0, tiled=True)

    above = jnp.zeros((2, 25, 256), jnp.float32)
    marked = above.at[:, 17, :].set(segment_index.astype(jnp.float32))

    def window(x, top):
        return lax.dynamic_slice_in_dim(jnp.concatenate([top, x, above], axis=1), 32 * block, 82, axis=1)

    mine = jnp.stack([window(capacity, above), window(source, marked), window(initial_state, above)])
    theirs = send(mine, PARTNER)
    outer = jnp.where(core == 0, mine[2, 0], mine[2, 1])
    facing = send(outer, FACING)
    facing_same = send(outer, FACING_SAME)
    chip4 = jnp.where(core == 0, jnp.concatenate([mine, theirs], axis=1), jnp.concatenate([theirs, mine], axis=1))
    before = jnp.where(core == 0, facing, facing_same)
    after = jnp.where(core == 0, facing_same, facing)
    state = jnp.concatenate([before[None], chip4[2], after[None]], axis=0)
    middle = state[1:-1, 1:-1]
    deeper = jnp.pad(middle, ((0, 0), (0, 0), (1, 1)))
    residual = (state[2:, 1:-1] + state[:-2, 1:-1] + state[1:-1, 2:] + state[1:-1, :-2]
                + deeper[:, :, 2:] + deeper[:, :, :-2] - 6.0 * middle + chip4[1, :, 1:-1])
    order = jnp.asarray(lane_order())

    def laid(x):
        return jnp.stack([jnp.dot(x, order[:, h * LANES:(h + 1) * LANES], precision=lax.Precision.HIGHEST)
                          for h in range(2)], axis=1)

    own_c, own_q = laid(chip4[0, :, 1:-1]), laid(residual)
    x_c, x_q = own_c[:, :, 8:72], own_q[:, :, 8:72]
    near, far = [], []
    for k in range(4):
        if k == 2:
            x_c, x_q = x_c[:, :, 8:56], x_q[:, :, 8:56]
        x_c, x_q = send(x_c, OUTWARD), send(x_q, OUTWARD)
        (near if k < 2 else far).append((x_c, x_q))
    edge = jnp.stack([own_c, own_q])[:, :, :, 16:64]
    end_cq = send(jnp.where(core == 0, edge[:, 3], edge[:, 0]), OUTWARD_5)
    near_c, near_q = (jnp.stack([b[j] for b in near]) for j in range(2))
    far_c, far_q = (jnp.stack([b[j] for b in far]) for j in range(2))
    got = (near_c, near_q, far_c, far_q, end_cq)
    passed = tuple(send(x, PARTNER) for x in got)

    first = jnp.where(block == 0, 1.0, 0.0)
    changes = jnp.concatenate([controls[:1], controls[1:] - controls[:-1]], axis=0) * first
    flags = jnp.zeros((1, SEGMENTS), jnp.float32).at[0, 0].set(jnp.where(core == 0, 1.0, 0.0)).at[0, 1].set(
        jnp.where(core == 1, 1.0, 0.0))
    steps = jnp.concatenate([changes, flags], axis=0)
    meta = jnp.stack([core.astype(jnp.int32), (core * 0).astype(jnp.int32)])
    ends = solve(meta, steps, own_c, own_q, *got, *passed)

    split = ends.reshape(SLICES * 2, 2, 16, 256)
    mixed = lax.all_to_all(split, ("tm", "core"), split_axis=0, concat_axis=0, tiled=True).reshape(2, 4, 2, 2, 16, 256)
    mixed = jnp.where(chip >= CHIPS // 2, mixed[::-1], mixed)
    whole = mixed.transpose(3, 0, 1, 2, 4, 5).reshape(2, 256, 256)
    return (whole + initial_state)[None]


def solution(mesh):
    split = Mesh(mesh.devices.reshape(8, CHIPS, 2), AXES)
    space = ("chip", "core")
    in_specs = (P(space, None, None), P(space, None, None), P(space, None, None), P("tm", None), P(space, None))
    return jax.shard_map(on_device, mesh=split, in_specs=in_specs, out_specs=P("tm", space, None, None), check_vma=False)
```

time: 689 us -> 164 us (0.24)
  starting transfers between devices: 285 us -> 27.9 us
  waiting for transfers between devices: 221 us -> 35.2 us
  other arithmetic: 109 us -> 8.94 us
  local copies, waits for them, and re-layouts: 56.3 us -> 5.71 us
  Pallas kernels: 0 us -> 47 us
  blocking collectives: 0 us -> 35.6 us
  between operations: 14 us -> 1.16 us
    ppermute x62 -> x17, starting transfers between devices: 279 us -> 27.9 us  [send(): return lax.ppermute(x, AXES, pairs)]
    all_gather x2 -> x0, waiting for transfers between devices: 101 us -> none  [run_chain(): every_term = lax.all_gather(correction_term[None], 'tm', axis=0, tiled=True)]
    ppermute x62 -> x17, waiting for transfers between devices: 120 us -> 35.2 us  [send(): return lax.ppermute(x, AXES, pairs)]
    select_n x27 -> x4, other arithmetic: 72.6 us -> 0.17 us  [the longest x1 0.1 us: on_device(): jnp.where(core == 0, jnp.concatenate([mine, theirs], axis=1), jnp.concate...]
    pallas_call x0 -> x1, Pallas kernels: none -> 47 us  [solve(): pl.pallas_call(main_kernel, out_shape=jax.ShapeDtypeStruct((SLICES, 4, 16...]
    slice x30 -> x4, local copies, waits for them, and re-layouts: 21.3 us -> 0.06 us  [the longest x2 0.03 us: on_device(): x_c, x_q = (x_c[:, :, 8:56], x_q[:, :, 8:56])]
    all_gather x0 -> x1, blocking collectives: none -> 21 us  [on_device(): controls = lax.all_gather(control, 'tm', axis=0, tiled=True)]
    dynamic_slice x14 -> x0, local copies, waits for them, and re-layouts: 15.1 us -> none  [chain_section(): lax.dynamic_index_in_dim(every_term, section_index, 0, keepdims=False)]
  transfers between devices with their start and end apart: 65 -> 17, of which waited for: 59 -> 9; matrix products, arithmetic and copies ran while one was open for 7% -> 5% of each run, Pallas kernels for 0% -> 0%
where the time goes in v1:
time: 164 us; the launch traced here: 163 us
  Pallas kernels  47 us (29%)
  blocking collectives  35.6 us (22%)
  waiting for transfers between devices  35.2 us (21%)
  starting transfers between devices  27.9 us (17%)
  other arithmetic  8.94 us (5%)
  local copies, waits for them, and re-layouts  5.71 us (3%)
  matrix products  1.7 us (1%)
    pallas_call x1, Pallas kernels, solve(): pl.pallas_call(main_kernel, out_shape=jax.ShapeDtypeStruct((SLICES, 4, 16...  47 us
    ppermute x17, waiting for transfers between devices, send(): return lax.ppermute(x, AXES, pairs)  35.2 us
    ppermute x17, starting transfers between devices, send(): return lax.ppermute(x, AXES, pairs)  27.9 us
    all_gather x1, blocking collectives, on_device(): controls = lax.all_gather(control, 'tm', axis=0, tiled=True)  21 us
    all_to_all x1, blocking collectives, on_device(): lax.all_to_all(split, ('tm', 'core'), split_axis=0, concat_axis=0, tiled=...  14.6 us
    another operation x4, other arithmetic  3.91 us
  transfers between devices with their start and end apart: 17, of which 9 were waited for; matrix products, arithmetic and copies ran while one was open for 5% of the time, Pallas kernels for 0%

profile of v1, /device:TPU:4, one launch (start us, length us, event | category | flops | bytes accessed | tf_op | source)
XLA Modules:
  0.0 163.2 jit_solution(15708098501445289335)
XLA Ops:
  0.7 1.3 fusion.12
  2.5 7.7 %collective-permute-start.1 = (f32[82,256]{1,0:T(8,128)S(1)}, f32[82,256]{1,0:T(8,128)S(1)}, u32[]{:S(2)}, u32[]{:S(2)}) collective-permute-start(f32[82,256]{1,0:T(8,128)S(1)} %fusion.19), channel_id=1, source_target_pairs={{1,3},{2,0},{3,5},{4,2},{5,7},{6,4},{7,9},{8,6},{9,11},{10,8},{11,... | collective-permute-start | bytes 251912 | tf_op jit(solution)/shard_map/ppermute | solution.py:44
  10.2 2.0 %collective-permute-start.2 = (f32[82,256]{1,0:T(8,128)S(1)}, f32[82,256]{1,0:T(8,128)S(1)}, u32[]{:S(2)}, u32[]{:S(2)}) collective-permute-start(f32[82,256]{1,0:T(8,128)S(1)} %fusion.19), channel_id=1, source_target_pairs={{1,2},{2,1},{3,4},{4,3},{5,6},{6,5},{7,8},{8,7},{9,10},{10,9},{11,... | collective-permute-start | bytes 251912 | tf_op jit(solution)/shard_map/ppermute | solution.py:44
  12.3 5.8 %collective-permute-done.2 = f32[82,256]{1,0:T(8,128)S(1)} collective-permute-done((f32[82,256]{1,0:T(8,128)S(1)}, f32[82,256]{1,0:T(8,128)S(1)}, u32[]{:S(2)}, u32[]{:S(2)}) %collective-permute-start.2) | collective-permute-done | bytes 84000 | tf_op jit(solution)/shard_map/ppermute | solution.py:44
  21.5 1.9 %collective-permute-start.5 = (f32[4,2,64,128]{3,2,1,0:T(8,128)S(1)}, f32[4,2,64,128]{3,2,1,0:T(8,128)S(1)}, u32[]{:S(2)}, u32[]{:S(2)}) collective-permute-start(f32[4,2,64,128]{3,2,1,0:T(8,128)S(1)} %fusion.8), channel_id=1, source_target_pairs={{0,2},{2,4},{3,1},{4,6},{5,3},{6,8},{7,5},{8,10},{9,7},{10,12},{11... | collective-permute-start | bytes 786440 | tf_op jit(solution)/shard_map/ppermute | solution.py:44
  23.5 1.9 %collective-permute-start.3 = (f32[4,2,64,128]{3,2,1,0:T(8,128)S(1)}, f32[4,2,64,128]{3,2,1,0:T(8,128)S(1)}, u32[]{:S(2)}, u32[]{:S(2)}) collective-permute-start(f32[4,2,64,128]{3,2,1,0:T(8,128)S(1)} %fusion.9), channel_id=1, source_target_pairs={{0,2},{2,4},{3,1},{4,6},{5,3},{6,8},{7,5},{8,10},{9,7},{10,12},{11... | collective-permute-start | bytes 786440 | tf_op jit(solution)/shard_map/ppermute | solution.py:44
  25.4 6.5 %collective-permute-done.5 = f32[4,2,64,128]{3,2,1,0:T(8,128)S(1)} collective-permute-done((f32[4,2,64,128]{3,2,1,0:T(8,128)S(1)}, f32[4,2,64,128]{3,2,1,0:T(8,128)S(1)}, u32[]{:S(2)}, u32[]{:S(2)}) %collective-permute-start.5) | collective-permute-done | bytes 262176 | tf_op jit(solution)/shard_map/ppermute | solution.py:44
  31.9 1.9 %collective-permute-start.6 = (f32[4,2,64,128]{3,2,1,0:T(8,128)S(1)}, f32[4,2,64,128]{3,2,1,0:T(8,128)S(1)}, u32[]{:S(2)}, u32[]{:S(2)}) collective-permute-start(f32[4,2,64,128]{3,2,1,0:T(8,128)S(1)} %collective-permute-done.5), channel_id=1, source_target_pairs={{0,2},{2,4},{3,1},{4,6},{5,3},{6,8},{7,5},{8,10},{9,7},{10,12},{11... | collective-permute-start | bytes 786440 | tf_op jit(solution)/shard_map/ppermute | solution.py:44
  33.8 21.0 %all-gather = f32[8,1,16]{2,1,0:T(1,128)S(1)} all-gather(f32[1,1,16]{2,1,0:T(1,128)S(1)} %bitcast.84), channel_id=1, replica_groups=mesh['tm'=8,'chip'=16,'core'=2] {'tm'}, dimensions={0}, use_global_device_ids=true | all-gather | bytes 576 | tf_op jit(solution)/shard_map/all_gather | solution.py:351
  54.8 1.9 %collective-permute-start.4 = (f32[4,2,64,128]{3,2,1,0:T(8,128)S(1)}, f32[4,2,64,128]{3,2,1,0:T(8,128)S(1)}, u32[]{:S(2)}, u32[]{:S(2)}) collective-permute-start(f32[4,2,64,128]{3,2,1,0:T(8,128)S(1)} %collective-permute-done.3), channel_id=1, source_target_pairs={{0,2},{2,4},{3,1},{4,6},{5,3},{6,8},{7,5},{8,10},{9,7},{10,12},{11... | collective-permute-start | bytes 786440 | tf_op jit(solution)/shard_map/ppermute | solution.py:44
  56.8 1.9 %collective-permute-start.9 = (f32[4,2,48,128]{3,2,1,0:T(8,128)S(1)}, f32[4,2,48,128]{3,2,1,0:T(8,128)S(1)}, u32[]{:S(2)}, u32[]{:S(2)}) collective-permute-start(f32[4,2,48,128]{3,2,1,0:T(8,128)S(1)} %slice.171), channel_id=1, source_target_pairs={{0,2},{2,4},{3,1},{4,6},{5,3},{6,8},{7,5},{8,10},{9,7},{10,12},{11... | collective-permute-start | bytes 589832 | tf_op jit(solution)/shard_map/ppermute | solution.py:44
  61.4 1.9 %fusion.22 = f32[1,1]{1,0:T(1,128)} fusion(pred[1,1]{1,0:T(4,128)(4,1)} %bitcast.7, f32[1,1]{1,0:T(1,128)} %bitcast.8, s32[]{:T(128)} %bitcast.9, f32[1,1]{1,0:T(1,128)} %bitcast.6), kind=kLoop, calls=%fused_computation.70 | loop fusion | flops 1 | bytes 17 | tf_op jit(solution)/shard_map/select.4
  63.3 1.4 scatter.11
  64.7 1.1 collective-permute-done.4
  65.8 1.9 %collective-permute-start.7 = (f32[4,2,48,128]{3,2,1,0:T(8,128)S(1)}, f32[4,2,48,128]{3,2,1,0:T(8,128)S(1)}, u32[]{:S(2)}, u32[]{:S(2)}) collective-permute-start(f32[4,2,48,128]{3,2,1,0:T(8,128)S(1)} %slice.170), channel_id=1, source_target_pairs={{0,2},{2,4},{3,1},{4,6},{5,3},{6,8},{7,5},{8,10},{9,7},{10,12},{11... | collective-permute-start | bytes 589832 | tf_op jit(solution)/shard_map/ppermute | solution.py:44
  67.9 1.9 %collective-permute-start.10 = (f32[4,2,48,128]{3,2,1,0:T(8,128)S(1)}, f32[4,2,48,128]{3,2,1,0:T(8,128)S(1)}, u32[]{:S(2)}, u32[]{:S(2)}) collective-permute-start(f32[4,2,48,128]{3,2,1,0:T(8,128)S(1)} %collective-permute-done.9), channel_id=1, source_target_pairs={{0,2},{2,4},{3,1},{4,6},{5,3},{6,8},{7,5},{8,10},{9,7},{10,12},{11... | collective-permute-start | bytes 589832 | tf_op jit(solution)/shard_map/ppermute | solution.py:44
  70.0 5.5 %collective-permute-done.7 = f32[4,2,48,128]{3,2,1,0:T(8,128)S(1)} collective-permute-done((f32[4,2,48,128]{3,2,1,0:T(8,128)S(1)}, f32[4,2,48,128]{3,2,1,0:T(8,128)S(1)}, u32[]{:S(2)}, u32[]{:S(2)}) %collective-permute-start.7) | collective-permute-done | bytes 196640 | tf_op jit(solution)/shard_map/ppermute | solution.py:44
  75.5 1.9 %collective-permute-start.8 = (f32[4,2,48,128]{3,2,1,0:T(8,128)S(1)}, f32[4,2,48,128]{3,2,1,0:T(8,128)S(1)}, u32[]{:S(2)}, u32[]{:S(2)}) collective-permute-start(f32[4,2,48,128]{3,2,1,0:T(8,128)S(1)} %collective-permute-done.7), channel_id=1, source_target_pairs={{0,2},{2,4},{3,1},{4,6},{5,3},{6,8},{7,5},{8,10},{9,7},{10,12},{11... | collective-permute-start | bytes 589832 | tf_op jit(solution)/shard_map/ppermute | solution.py:44
  78.2 7.0 %collective-permute-done.8 = f32[4,2,48,128]{3,2,1,0:T(8,128)S(1)} collective-permute-done((f32[4,2,48,128]{3,2,1,0:T(8,128)S(1)}, f32[4,2,48,128]{3,2,1,0:T(8,128)S(1)}, u32[]{:S(2)}, u32[]{:S(2)}) %collective-permute-start.8) | collective-permute-done | bytes 196640 | tf_op jit(solution)/shard_map/ppermute | solution.py:44
  85.3 1.0 fusion.20
  86.3 1.9 %collective-permute-start.11 = (f32[2,2,48,128]{3,2,1,0:T(8,128)S(1)}, f32[2,2,48,128]{3,2,1,0:T(8,128)S(1)}, u32[]{:S(2)}, u32[]{:S(2)}) collective-permute-start(f32[2,2,48,128]{3,2,1,0:T(8,128)S(1)} %fusion.18), channel_id=1, source_target_pairs={{0,10},{2,12},{4,14},{6,144},{8,146},{10,148},{11,1},{12,150},{13,... | collective-permute-start | bytes 294920 | tf_op jit(solution)/shard_map/ppermute | solution.py:44
  88.8 8.3 %collective-permute-done.11.end_cq = f32[2,2,48,128]{3,2,1,0:T(8,128)S(1)} collective-permute-done((f32[2,2,48,128]{3,2,1,0:T(8,128)S(1)}, f32[2,2,48,128]{3,2,1,0:T(8,128)S(1)}, u32[]{:S(2)}, u32[]{:S(2)}) %collective-permute-start.11) | collective-permute-done | bytes 98336 | tf_op jit(solution)/shard_map/ppermute | solution.py:44
  99.7 47.0 %parareal.1 = f32[8,4,16,256]{3,2,1,0:T(8,128)} custom-call(s32[2]{0:T(128)} %pad_add_fusion.meta, f32[9,16]{1,0:T(8,128)} %pad_maximum_fusion.10.steps, f32[4,2,80,128]{3,2,1,0:T(8,128)} %get-tuple-element.50.own_c, f32[4,2,80,128]{3,2,1,0:T(8,128)} %get-tuple-element.44.own_q, f32[2,4,2,64,128]{4,3,2,1,0:T(8,128)} %copy-done.2, ...), custom_call_target="tpu_custom_call" | custom-call | tf_op jit(solution)/shard_map/parareal/pallas_call | solution.py:331
  146.7 14.6 %all_to_all.5 = f32[16,2,16,256]{3,2,1,0:T(8,128)S(1)} all-to-all(f32[16,2,16,256]{3,2,1,0:T(8,128)} %bitcast.74), channel_id=1, replica_groups=mesh['tm'=8,'chip'=16,'core'=2] {'tm','core'}, dimensions={0} | all-to-all | bytes 1048576 | tf_op jit(solution)/shard_map/all_to_all | solution.py:402
  (83 shorter events, 12.6 us)
Async XLA Ops:
  2.4 15.9 %collective-permute-start = (f32[3,2,82,256]{3,1,2,0:T(2,128)S(1)}, f32[3,2,82,256]{3,1,2,0:T(2,128)S(1)}, u32[]{:S(2)}, u32[]{:S(2)}) collective-permute-start(f32[3,2,82,256]{3,1,2,0:T(2,128)S(1)} %copy.14), channel_id=1, source_target_pairs={{0,1},{1,0},{2,3},{3,2},{4,5},{5,4},{6,7},{7,6},{8,9},{9,8},{10,11... | collective-permute-start | bytes 1511432 | tf_op jit(solution)/shard_map/ppermute | solution.py:44
  2.5 9.9 %collective-permute-start.1 = (f32[82,256]{1,0:T(8,128)S(1)}, f32[82,256]{1,0:T(8,128)S(1)}, u32[]{:S(2)}, u32[]{:S(2)}) collective-permute-start(f32[82,256]{1,0:T(8,128)S(1)} %fusion.19), channel_id=1, source_target_pairs={{1,3},{2,0},{3,5},{4,2},{5,7},{6,4},{7,9},{8,6},{9,11},{10,8},{11,... | collective-permute-start | bytes 251912 | tf_op jit(solution)/shard_map/ppermute | solution.py:44
  10.2 8.0 %collective-permute-start.2 = (f32[82,256]{1,0:T(8,128)S(1)}, f32[82,256]{1,0:T(8,128)S(1)}, u32[]{:S(2)}, u32[]{:S(2)}) collective-permute-start(f32[82,256]{1,0:T(8,128)S(1)} %fusion.19), channel_id=1, source_target_pairs={{1,2},{2,1},{3,4},{4,3},{5,6},{6,5},{7,8},{8,7},{9,10},{10,9},{11,... | collective-permute-start | bytes 251912 | tf_op jit(solution)/shard_map/ppermute | solution.py:44
  20.6 13.2 %copy-start.13 = (f32[1,16]{1,0:T(1,128)S(1)}, f32[1,16]{1,0:T(1,128)}, u32[]{:S(2)}) copy-start(f32[1,16]{1,0:T(1,128)} %param.16) | copy-start | bytes 196
  21.5 10.4 %collective-permute-start.5 = (f32[4,2,64,128]{3,2,1,0:T(8,128)S(1)}, f32[4,2,64,128]{3,2,1,0:T(8,128)S(1)}, u32[]{:S(2)}, u32[]{:S(2)}) collective-permute-start(f32[4,2,64,128]{3,2,1,0:T(8,128)S(1)} %fusion.8), channel_id=1, source_target_pairs={{0,2},{2,4},{3,1},{4,6},{5,3},{6,8},{7,5},{8,10},{9,7},{10,12},{11... | collective-permute-start | bytes 786440 | tf_op jit(solution)/shard_map/ppermute | solution.py:44
  23.5 31.3 %collective-permute-start.3 = (f32[4,2,64,128]{3,2,1,0:T(8,128)S(1)}, f32[4,2,64,128]{3,2,1,0:T(8,128)S(1)}, u32[]{:S(2)}, u32[]{:S(2)}) collective-permute-start(f32[4,2,64,128]{3,2,1,0:T(8,128)S(1)} %fusion.9), channel_id=1, source_target_pairs={{0,2},{2,4},{3,1},{4,6},{5,3},{6,8},{7,5},{8,10},{9,7},{10,12},{11... | collective-permute-start | bytes 786440 | tf_op jit(solution)/shard_map/ppermute | solution.py:44
  31.9 24.8 %collective-permute-start.6 = (f32[4,2,64,128]{3,2,1,0:T(8,128)S(1)}, f32[4,2,64,128]{3,2,1,0:T(8,128)S(1)}, u32[]{:S(2)}, u32[]{:S(2)}) collective-permute-start(f32[4,2,64,128]{3,2,1,0:T(8,128)S(1)} %collective-permute-done.5), channel_id=1, source_target_pairs={{0,2},{2,4},{3,1},{4,6},{5,3},{6,8},{7,5},{8,10},{9,7},{10,12},{11... | collective-permute-start | bytes 786440 | tf_op jit(solution)/shard_map/ppermute | solution.py:44
  54.8 11.0 %collective-permute-start.4 = (f32[4,2,64,128]{3,2,1,0:T(8,128)S(1)}, f32[4,2,64,128]{3,2,1,0:T(8,128)S(1)}, u32[]{:S(2)}, u32[]{:S(2)}) collective-permute-start(f32[4,2,64,128]{3,2,1,0:T(8,128)S(1)} %collective-permute-done.3), channel_id=1, source_target_pairs={{0,2},{2,4},{3,1},{4,6},{5,3},{6,8},{7,5},{8,10},{9,7},{10,12},{11... | collective-permute-start | bytes 786440 | tf_op jit(solution)/shard_map/ppermute | solution.py:44
  56.8 11.1 %collective-permute-start.9 = (f32[4,2,48,128]{3,2,1,0:T(8,128)S(1)}, f32[4,2,48,128]{3,2,1,0:T(8,128)S(1)}, u32[]{:S(2)}, u32[]{:S(2)}) collective-permute-start(f32[4,2,48,128]{3,2,1,0:T(8,128)S(1)} %slice.171), channel_id=1, source_target_pairs={{0,2},{2,4},{3,1},{4,6},{5,3},{6,8},{7,5},{8,10},{9,7},{10,12},{11... | collective-permute-start | bytes 589832 | tf_op jit(solution)/shard_map/ppermute | solution.py:44
  65.8 9.7 %collective-permute-start.7 = (f32[4,2,48,128]{3,2,1,0:T(8,128)S(1)}, f32[4,2,48,128]{3,2,1,0:T(8,128)S(1)}, u32[]{:S(2)}, u32[]{:S(2)}) collective-permute-start(f32[4,2,48,128]{3,2,1,0:T(8,128)S(1)} %slice.170), channel_id=1, source_target_pairs={{0,2},{2,4},{3,1},{4,6},{5,3},{6,8},{7,5},{8,10},{9,7},{10,12},{11... | collective-permute-start | bytes 589832 | tf_op jit(solution)/shard_map/ppermute | solution.py:44
  67.9 9.7 %collective-permute-start.10 = (f32[4,2,48,128]{3,2,1,0:T(8,128)S(1)}, f32[4,2,48,128]{3,2,1,0:T(8,128)S(1)}, u32[]{:S(2)}, u32[]{:S(2)}) collective-permute-start(f32[4,2,48,128]{3,2,1,0:T(8,128)S(1)} %collective-permute-done.9), channel_id=1, source_target_pairs={{0,2},{2,4},{3,1},{4,6},{5,3},{6,8},{7,5},{8,10},{9,7},{10,12},{11... | collective-permute-start | bytes 589832 | tf_op jit(solution)/shard_map/ppermute | solution.py:44
  69.8 15.3 %copy-start.1 = (f32[2,4,2,64,128]{4,3,2,1,0:T(8,128)}, f32[2,4,2,64,128]{4,3,2,1,0:T(8,128)S(1)}, u32[]{:S(2)}) copy-start(f32[2,4,2,64,128]{4,3,2,1,0:T(8,128)S(1)} %pad_maximum_fusion.2.near_q) | copy-start | bytes 1572868
  69.9 28.6 %collective-permute-start.13 = (f32[2,4,2,64,128]{4,3,2,1,0:T(8,128)S(1)}, f32[2,4,2,64,128]{4,3,2,1,0:T(8,128)S(1)}, u32[]{:S(2)}, u32[]{:S(2)}) collective-permute-start(f32[2,4,2,64,128]{4,3,2,1,0:T(8,128)S(1)} %pad_maximum_fusion.2.near_q), channel_id=1, source_target_pairs={{0,1},{1,0},{2,3},{3,2},{4,5},{5,4},{6,7},{7,6},{8,9},{9,8},{10,11... | collective-permute-start | bytes 1572872 | tf_op jit(solution)/shard_map/ppermute | solution.py:44
  75.5 9.7 %collective-permute-start.8 = (f32[4,2,48,128]{3,2,1,0:T(8,128)S(1)}, f32[4,2,48,128]{3,2,1,0:T(8,128)S(1)}, u32[]{:S(2)}, u32[]{:S(2)}) collective-permute-start(f32[4,2,48,128]{3,2,1,0:T(8,128)S(1)} %collective-permute-done.7), channel_id=1, source_target_pairs={{0,2},{2,4},{3,1},{4,6},{5,3},{6,8},{7,5},{8,10},{9,7},{10,12},{11... | collective-permute-start | bytes 589832 | tf_op jit(solution)/shard_map/ppermute | solution.py:44
  77.4 8.8 %copy-start.2 = (f32[2,4,2,64,128]{4,3,2,1,0:T(8,128)}, f32[2,4,2,64,128]{4,3,2,1,0:T(8,128)S(1)}, u32[]{:S(2)}) copy-start(f32[2,4,2,64,128]{4,3,2,1,0:T(8,128)S(1)} %pad_maximum_fusion.1.near_c) | copy-start | bytes 1572868
  77.4 21.0 %collective-permute-start.12 = (f32[2,4,2,64,128]{4,3,2,1,0:T(8,128)S(1)}, f32[2,4,2,64,128]{4,3,2,1,0:T(8,128)S(1)}, u32[]{:S(2)}, u32[]{:S(2)}) collective-permute-start(f32[2,4,2,64,128]{4,3,2,1,0:T(8,128)S(1)} %pad_maximum_fusion.1.near_c), channel_id=1, source_target_pairs={{0,1},{1,0},{2,3},{3,2},{4,5},{5,4},{6,7},{7,6},{8,9},{9,8},{10,11... | collective-permute-start | bytes 1572872 | tf_op jit(solution)/shard_map/ppermute | solution.py:44
  77.6 8.6 %copy-start.3 = (f32[2,4,2,48,128]{4,3,2,1,0:T(8,128)}, f32[2,4,2,48,128]{4,3,2,1,0:T(8,128)S(1)}, u32[]{:S(2)}) copy-start(f32[2,4,2,48,128]{4,3,2,1,0:T(8,128)S(1)} %pad_maximum_fusion.4.far_q) | copy-start | bytes 1179652
  77.6 20.8 %collective-permute-start.15 = (f32[2,4,2,48,128]{4,3,2,1,0:T(8,128)S(1)}, f32[2,4,2,48,128]{4,3,2,1,0:T(8,128)S(1)}, u32[]{:S(2)}, u32[]{:S(2)}) collective-permute-start(f32[2,4,2,48,128]{4,3,2,1,0:T(8,128)S(1)} %pad_maximum_fusion.4.far_q), channel_id=1, source_target_pairs={{0,1},{1,0},{2,3},{3,2},{4,5},{5,4},{6,7},{7,6},{8,9},{9,8},{10,11... | collective-permute-start | bytes 1179656 | tf_op jit(solution)/shard_map/ppermute | solution.py:44
  85.2 13.3 %collective-permute-start.14 = (f32[2,4,2,48,128]{4,3,2,1,0:T(8,128)S(1)}, f32[2,4,2,48,128]{4,3,2,1,0:T(8,128)S(1)}, u32[]{:S(2)}, u32[]{:S(2)}) collective-permute-start(f32[2,4,2,48,128]{4,3,2,1,0:T(8,128)S(1)} %pad_maximum_fusion.3.far_c), channel_id=1, source_target_pairs={{0,1},{1,0},{2,3},{3,2},{4,5},{5,4},{6,7},{7,6},{8,9},{9,8},{10,11... | collective-permute-start | bytes 1179656 | tf_op jit(solution)/shard_map/ppermute | solution.py:44
  86.3 10.9 %collective-permute-start.11 = (f32[2,2,48,128]{3,2,1,0:T(8,128)S(1)}, f32[2,2,48,128]{3,2,1,0:T(8,128)S(1)}, u32[]{:S(2)}, u32[]{:S(2)}) collective-permute-start(f32[2,2,48,128]{3,2,1,0:T(8,128)S(1)} %fusion.18), channel_id=1, source_target_pairs={{0,10},{2,12},{4,14},{6,144},{8,146},{10,148},{11,1},{12,150},{13,... | collective-permute-start | bytes 294920 | tf_op jit(solution)/shard_map/ppermute | solution.py:44
  97.1 2.2 %copy-start.11 = (f32[2,2,48,128]{3,2,1,0:T(8,128)}, f32[2,2,48,128]{3,2,1,0:T(8,128)S(1)}, u32[]{:S(2)}) copy-start(f32[2,2,48,128]{3,2,1,0:T(8,128)S(1)} %collective-permute-done.11.end_cq) | copy-start | bytes 294916
  97.1 1.3 collective-permute-start.16
  98.5 1.1 copy-start.8
  98.5 1.2 copy-start.9
  (7 other events, 6.6 us)

commit v2 on v1

v2 whole, which is shorter than its diff:
```python
import jax
import jax.numpy as jnp
import numpy as np
from jax import lax
from jax.experimental import pallas as pl
from jax.experimental.pallas import tpu as pltpu
from jax.sharding import Mesh
from jax.sharding import PartitionSpec as P

SWEEPS = 6
SLICES = 8
SEGMENTS = 16
COARSE = 0.08
AXES = ("tm", "chip", "core")
CHIPS = 16
PLANES = 38
ROWS = 72
OWN = 24
MOST = 112
LANES = 128
REACH = 17


def device_pairs(target):
    pairs = []
    for t in range(8):
        for chip in range(CHIPS):
            for core in range(2):
                to = target(chip, core)
                if to is None or not 0 <= to[0] < CHIPS:
                    continue
                t_to = t if chip // 8 == to[0] // 8 else t ^ 4
                pairs.append(((t * CHIPS + chip) * 2 + core, (t_to * CHIPS + to[0]) * 2 + to[1]))
    return pairs


PARTNER = device_pairs(lambda chip, core: (chip, 1 - core))
OUTWARD = device_pairs(lambda chip, core: (chip + 1 - 2 * core, core))
OUTWARD_5 = device_pairs(lambda chip, core: (chip + 5 - 10 * core, core))
FACING = device_pairs(lambda chip, core: (chip - 1 + 2 * core, 1 - core))
FACING_SAME = device_pairs(lambda chip, core: (chip - 1 + 2 * core, core))


def send(x, pairs):
    return lax.ppermute(x, AXES, pairs)


def lane_order():
    order = np.zeros((256, 256), np.float32)
    for z in range(256):
        order[z, (z % 2) * LANES + z // 2] = 1.0
    return order


def tiles(r):
    out = {}
    for p in range(REACH - r, REACH + 4 + r):
        rho = -(-(r - max(0, REACH - p, p - REACH - 3)) // 4)
        for k in range(2 + rho):
            out.setdefault(OWN - 4 * rho + 8 * k, []).append(p)
    return sorted(out.items())


def main_kernel(controls, *refs):
    (own_c, own_q), blocks, (order, out) = refs[:2], refs[2:20], refs[20:22]
    sig, rd, q, v, wa, wb, ua, ub, e, le, hh, total, jumps, segs, ends, sems = refs[22:]
    core, chip, tm = lax.axis_index("core"), lax.axis_index("chip"), lax.axis_index("tm")
    zero = tm >> 5
    trips = zero + 1
    at_edge = jnp.where(chip >= CHIPS // 2, tm ^ 4, tm) == 0

    copies = []

    def copy(src, dst):
        c = pltpu.make_async_copy(src, dst, sems.at[len(copies)])
        c.start()
        copies.append(c)

    half = pl.multiple_of(core * 16, 8)
    for f, (own, dst) in enumerate(((own_c, sig), (own_q, q))):
        copy(own.at[:, :, pl.ds(half, 64), :], dst.at[pl.ds(REACH, 4), :, pl.ds(0, 64), :])
        for mine in range(2):
            side = 1 - core if mine == 1 else core
            group = blocks[9 * mine:9 * mine + 9]
            for k in range(1, 5):
                b = group[2 * (k - 1) + f]
                p = REACH - 4 * k + side * (8 * k)
                if k <= 2:
                    copy(b.at[:, :, pl.ds(half, 48), :], dst.at[pl.ds(p, 4), :, pl.ds(OWN - 16, 48), :])
                    if k == 1 and f == 1:
                        copy(b.at[:, :, pl.ds(8, 8), :], dst.at[pl.ds(p, 4), :, pl.ds(0, 8), :])
                else:
                    copy(b.at[:, :, pl.ds(half, 32), :], dst.at[pl.ds(p, 4), :, pl.ds(OWN - 8, 32), :])
            copy(group[8].at[f, :, pl.ds(half, 32), :], dst.at[(PLANES - 1) * side, :, pl.ds(OWN - 8, 32), :])
    for c in copies:
        c.wait()

    lane = lax.broadcasted_iota(jnp.int32, (8, LANES), 1)
    row = lax.broadcasted_iota(jnp.int32, (8, LANES), 0)
    first, last = lane == 0, lane == LANES - 1

    def take_segments(p, _):
        for h in range(2):
            segs[h, pl.ds(p, 1), :] = q[p, h, pl.ds(16 * (1 - core), 1), :]
        return 0

    lax.fori_loop(0, PLANES, take_segments, 0)
    here = [jnp.where(at_edge & (core == c), 1.0, 0.0) for c in range(2)]
    for h in range(2):
        s = segs[h]
        acc = [jnp.zeros_like(s) for _ in range(SLICES)]
        for m in range(SEGMENTS):
            hit = s == jnp.float32(m)
            for n in range(SLICES):
                change = controls[n, m] - controls[n - 1, m] if n > 0 else controls[n, m]
                acc[n] = jnp.where(hit, change, acc[n])
        for n in range(SLICES):
            jumps[0, n, h] = acc[n] * here[0]
            if n < 3:
                jumps[1, n, h] = acc[n] * here[1] if n < 2 else jnp.zeros_like(s)

    def step(*stages):
        blocks, room = [], 0
        for stage, part in stages:
            part = list(part)
            while part:
                if room < 8:
                    blocks.append([])
                    room = MOST
                blocks[-1].append((stage, part[:room]))
                part, room = part[room:], room - min(room, len(part))
        for block in blocks:
            def body(_, carry, block=block):
                stores = []
                for stage, part in block:
                    stage(stores, part)
                for ref, p, h, y, value in stores:
                    ref[p, h, pl.ds(y, 8), :] = value
                return carry

            lax.fori_loop(0, trips, body, 0)

    def loader():
        cache = {}

        def load(ref, p, h, y, base=0):
            key = (id(ref), p, h, y)
            if key not in cache:
                cache[key] = ref[base + p, h, pl.ds(zero + y, 8), :]
            return cache[key]

        return load

    def around(ref, load, p, y, base=0):
        even, odd = load(ref, p, 0, y, base), load(ref, p, 1, y, base)
        z = (odd + jnp.where(first, 0.0, pltpu.roll(odd, 1, 1)), even + jnp.where(last, 0.0, pltpu.roll(even, LANES - 1, 1)))
        return [z[h] + (load(ref, p, h, y - 1, base) + load(ref, p, h, y + 1, base))
                + (load(ref, p - 1, h, y, base) + load(ref, p + 1, h, y, base)) for h in range(2)]

    def cells(r):
        for y, planes in tiles(r):
            for p in planes:
                yield y, p

    def jump(n, p, h, y, both):
        result = None
        for which, at in ((0, OWN), (1, OWN - 16)):
            if y <= at < y + 8 and (which == 0 or both):
                value = jnp.where(row == at - y, jumps[which, n, h, pl.ds(p, 1), :], 0.0)
                result = value if result is None else result + value
        return result

    def setup(stores, part):
        load = loader()
        for y, p in part:
            for h in range(2):
                c = load(sig, p, h, y)
                inside = c > 0.0
                c = jnp.where(inside, c, 1.0)
                s = jnp.where(inside, COARSE / c, 0.0)
                d = jnp.where(inside, 1.0 / (c + 6.0), 0.0)
                value = load(q, p, h, y)
                change = jump(0, p, h, y, True)
                if change is not None:
                    value = value + change
                    stores.append((q, p, h, zero + y, value))
                stores += [(sig, p, h, zero + y, s), (rd, p, h, zero + y, d), (v, p, h, zero + y, s * value),
                           (wa, p, h, zero + y, d * value)]

    def clear(stores, part):
        nothing = jnp.zeros((8, LANES), jnp.float32)
        for p in range(REACH - 7, REACH + 11):
            for h in range(2):
                for y in range(OWN - 16, OWN + 32, 8):
                    stores.append((hh, p, h, y, nothing))
        for p in range(4):
            for h in range(2):
                stores += [(total, p, h, 0, nothing), (total, p, h, 8, nothing)]

    def advance(n, r, old, new, both):
        def stage(stores, part):
            load = loader()
            for y, p in part:
                sums = around(v, load, p, y, old)
                for h in range(2):
                    value = load(q, p, h, y) + (sums[h] - 6.0 * load(v, p, h, y))
                    change = jump(n, p, h, y, both)
                    if change is not None:
                        value = value + change
                    stores.append((q, p, h, zero + y, value))
                    if new is not None:
                        stores += [(v, new + p, h, zero + y, load(sig, p, h, y) * value),
                                   (wa, p, h, zero + y, load(rd, p, h, y) * value)]
        return stage, cells(r)

    def second_order(r):
        def stage(stores, part):
            load = loader()
            for y, p in part:
                sums = around(e, load, p, y)
                for h in range(2):
                    value = sums[h] - 6.0 * load(e, p, h, y)
                    stores += [(le, p, h, zero + y, value), (ua, p, h, zero + y, load(rd, p, h, y) * value)]
        return stage, cells(r)

    def with_source(stores, part):
        load = loader()
        for y, p in part:
            for h in range(2):
                value = load(le, p, h, y) + load(q, p, h, y)
                stores += [(le, p, h, zero + y, value), (ua, p, h, zero + y, load(rd, p, h, y) * value)]

    def sweep(r, src, dst, source):
        def stage(stores, part):
            load = loader()
            for y, p in part:
                sums = around(src, load, p, y)
                for h in range(2):
                    stores.append((dst, p, h, zero + y, load(rd, p, h, y) * (load(source, p, h, y) + sums[h])))
        return stage, cells(r)

    def finish_first(initial, r, src):
        def stage(stores, part):
            load = loader()
            for y, p in part:
                sums = around(src, load, p, y)
                for h in range(2):
                    value = load(rd, p, h, y) * (load(q, p, h, y) + sums[h])
                    s = load(sig, p, h, y)
                    if initial:
                        value = value - s * load(q, p, h, y)
                    else:
                        value = load(e, p, h, y) + (value + s * (load(le, p, h, y) - load(q, p, h, y)))
                    stores.append((e, p, h, zero + y, value))
        return stage, cells(r)

    def finish_second(r, src, old, new):
        def stage(stores, part):
            load = loader()
            for y, p in part:
                sums = around(src, load, p, y)
                around_h = around(hh, load, p, y, old)
                for h in range(2):
                    value = load(rd, p, h, y) * (load(le, p, h, y) + sums[h])
                    coarse = around_h[h] - 6.0 * load(hh, p, h, y)
                    if new is not None:
                        coarse = coarse - load(le, p, h, y)
                    value = load(hh, p, h, y) + (value + load(sig, p, h, y) * coarse)
                    if new is not None:
                        stores.append((hh, new + p, h, zero + y, value))
                    else:
                        value = value + total[p - REACH, h, pl.ds(y - OWN, 8), :] + load(e, p, h, y)
                        stores.append((ends, (SLICES - 1) * 4 + p - REACH, h, y - OWN, value))
        return stage, cells(r)

    def close(n, old):
        def stage(stores, part):
            for y, p in part:
                for h in range(2):
                    value = v[old + p, h, pl.ds(y, 8), :] + total[p - REACH, h, pl.ds(y - OWN, 8), :]
                    stores.append((total, p - REACH, h, y - OWN, value))
                    value = value + e[p, h, pl.ds(y, 8), :] + hh[old + p, h, pl.ds(y, 8), :]
                    stores.append((ends, (n - 1) * 4 + p - REACH, h, y - OWN, value))
        return stage, cells(0)

    def sweeps(n, r_w, r_u, old, new, initial=False):
        w, u = (wa, wb), (ua, ub)
        for k in range(SWEEPS - 1):
            stages = []
            if r_w is not None:
                stages.append(sweep(r_w - k, *w, q) if k < SWEEPS - 2 else finish_first(initial, r_w - k, w[0]))
            if r_u is not None:
                stages.append(sweep(r_u - k, *u, le) if k < SWEEPS - 2 else finish_second(r_u - k, u[0], old, new))
            step(*stages)
            w, u = w[::-1], u[::-1]

    step((setup, cells(17)), (clear, [None]))
    sweeps(0, 16, None, None, None, True)
    for start in range(1, SLICES - 1, 2):
        def slice_pair(j, carry, start=start):
            n = start + j
            old, new = PLANES * j, PLANES * (1 - j)
            step(close(n, old), second_order(12 - start), advance(n, 17 - start, old, new, start == 1))
            sweeps(n, 16 - start, 11 - start, old, new)
            return carry

        lax.fori_loop(0, 2, slice_pair, 0)
    step(close(SLICES - 1, 0), second_order(5), advance(SLICES - 1, 5, 0, None, False))
    step((with_source, cells(5)))
    sweeps(SLICES - 1, None, 4, 0, None)

    both = jnp.concatenate([ends[:, h].reshape(SLICES * 4 * 16, LANES) for h in range(2)], axis=1)
    whole = lax.dot_general(both, order[...], (((1,), (1,)), ((), ())), precision=lax.Precision.HIGHEST,
                            preferred_element_type=jnp.float32)
    out[...] = whole.reshape(SLICES, 4, 16, 256)


def solve(controls, *blocks):
    field = pltpu.VMEM((PLANES, 2, ROWS, LANES), jnp.float32)
    two = pltpu.VMEM((2 * PLANES, 2, ROWS, LANES), jnp.float32)
    any_space = pl.BlockSpec(memory_space=pl.ANY)
    smem = pl.BlockSpec(memory_space=pltpu.SMEM)
    vmem = pl.BlockSpec(memory_space=pltpu.VMEM)
    return pl.pallas_call(
        main_kernel,
        out_shape=jax.ShapeDtypeStruct((SLICES, 4, 16, 256), jnp.float32),
        in_specs=[smem] + [any_space] * len(blocks) + [vmem],
        out_specs=vmem,
        scratch_shapes=[field] * 3 + [two] + [field] * 6 + [two] + [
            pltpu.VMEM((4, 2, 16, LANES), jnp.float32),
            pltpu.VMEM((2, SLICES, 2, 40, LANES), jnp.float32),
            pltpu.VMEM((2, 40, LANES), jnp.float32),
            pltpu.VMEM((SLICES * 4, 2, 16, LANES), jnp.float32),
            pltpu.SemaphoreType.DMA((24,)),
        ],
        compiler_params=pltpu.CompilerParams(vmem_limit_bytes=60 << 20),
        name="parareal",
    )(controls, *blocks, jnp.asarray(lane_order()))


def on_device(initial_state, capacity, source, control, segment_index):
    tm, chip, core = lax.axis_index("tm"), lax.axis_index("chip"), lax.axis_index("core")
    block = jnp.where(chip >= CHIPS // 2, tm ^ 4, tm)
    controls = lax.all_to_all(jnp.broadcast_to(control, (SLICES, SEGMENTS)), "tm", split_axis=0, concat_axis=0, tiled=True)

    above = jnp.zeros((2, 25, 256), jnp.float32)
    marked = above.at[:, 17, :].set(segment_index.astype(jnp.float32))

    def window(x, top):
        return lax.dynamic_slice_in_dim(jnp.concatenate([top, x, above], axis=1), 32 * block, 82, axis=1)

    mine = jnp.stack([window(capacity, above), window(source, marked), window(initial_state, above)])
    theirs = send(mine, PARTNER)
    outer = jnp.where(core == 0, mine[2, 0], mine[2, 1])
    facing = send(outer, FACING)
    facing_same = send(outer, FACING_SAME)
    chip4 = jnp.where(core == 0, jnp.concatenate([mine, theirs], axis=1), jnp.concatenate([theirs, mine], axis=1))
    before = jnp.where(core == 0, facing, facing_same)
    after = jnp.where(core == 0, facing_same, facing)
    state = jnp.concatenate([before[None], chip4[2], after[None]], axis=0)
    middle = state[1:-1, 1:-1]
    deeper = jnp.pad(middle, ((0, 0), (0, 0), (1, 1)))
    residual = (state[2:, 1:-1] + state[:-2, 1:-1] + state[1:-1, 2:] + state[1:-1, :-2]
                + deeper[:, :, 2:] + deeper[:, :, :-2] - 6.0 * middle + chip4[1, :, 1:-1])
    order = jnp.asarray(lane_order())

    def laid(x):
        return jnp.stack([jnp.dot(x, order[:, h * LANES:(h + 1) * LANES], precision=lax.Precision.HIGHEST)
                          for h in range(2)], axis=1)

    own_c, own_q = laid(chip4[0, :, 1:-1]), laid(residual)
    x_c, x_q = own_c[:, :, 8:72], own_q[:, :, 8:72]
    got = []
    for k in range(4):
        if k == 2:
            x_c, x_q = x_c[:, :, 8:56], x_q[:, :, 8:56]
        x_c, x_q = send(x_c, OUTWARD), send(x_q, OUTWARD)
        got += [x_c, x_q]
    edge = jnp.stack([own_c, own_q])[:, :, :, 16:64]
    got.append(send(jnp.where(core == 0, edge[:, 3], edge[:, 0]), OUTWARD_5))
    passed = [send(x, PARTNER) for x in got]
    ends = solve(controls, own_c, own_q, *got, *passed)

    split = ends.reshape(SLICES * 2, 2, 16, 256)
    mixed = lax.all_to_all(split, ("tm", "core"), split_axis=0, concat_axis=0, tiled=True).reshape(2, 4, 2, 2, 16, 256)
    mixed = jnp.where(chip >= CHIPS // 2, mixed[::-1], mixed)
    whole = mixed.transpose(3, 0, 1, 2, 4, 5).reshape(2, 256, 256)
    return (whole + initial_state)[None]


def solution(mesh):
    split = Mesh(mesh.devices.reshape(8, CHIPS, 2), AXES)
    space = ("chip", "core")
    in_specs = (P(space, None, None), P(space, None, None), P(space, None, None), P("tm", None), P(space, None))
    return jax.shard_map(on_device, mesh=split, in_specs=in_specs, out_specs=P("tm", space, None, None), check_vma=False)
```

time: 164 us -> 133 us (0.81)
  Pallas kernels: 47 us -> 33.4 us
  blocking collectives: 35.6 us -> 28.7 us
  other arithmetic: 8.94 us -> 4.36 us
  waiting for transfers between devices: 35.2 us -> 31.6 us
  local copies, waits for them, and re-layouts: 5.71 us -> 3.27 us
    all_gather x1 -> x0, blocking collectives: 21 us -> none  [on_device(): controls = lax.all_gather(control, 'tm', axis=0, tiled=True)]
    all_to_all x0 -> x1, blocking collectives: none -> 14.3 us  [on_device(): lax.all_to_all(jnp.broadcast_to(control, (SLICES, SEGMENTS)), 'tm', split...]
    pallas_call x1, Pallas kernels: 47 us -> 33.4 us  [solve(): pl.pallas_call(main_kernel, out_shape=jax.ShapeDtypeStruct((SLICES, 4, 16...]
    another operation x9 -> x1, other arithmetic: 4.62 us -> 0.68 us
    ppermute x17 -> x21, waiting for transfers between devices: 35.2 us -> 31.6 us  [send(): return lax.ppermute(x, AXES, pairs)]
    ppermute x17 -> x21, starting transfers between devices: 27.9 us -> 29 us  [send(): return lax.ppermute(x, AXES, pairs)]
  transfers between devices with their start and end apart: 17 -> 21, of which waited for: 9 -> 11; matrix products, arithmetic and copies ran while one was open for 5% -> 1% of each run, Pallas kernels for 0% -> 0%
where the time goes in v2:
time: 133 us
  Pallas kernels  33.4 us (25%)
  waiting for transfers between devices  31.6 us (24%)
  starting transfers between devices  29 us (22%)
  blocking collectives  28.7 us (22%)
  other arithmetic  4.36 us (3%)
  local copies, waits for them, and re-layouts  3.27 us (2%)
  matrix products  1.7 us (1%)
    pallas_call x1, Pallas kernels, solve(): pl.pallas_call(main_kernel, out_shape=jax.ShapeDtypeStruct((SLICES, 4, 16...  33.4 us
    ppermute x21, waiting for transfers between devices, send(): return lax.ppermute(x, AXES, pairs)  31.6 us
    ppermute x21, starting transfers between devices, send(): return lax.ppermute(x, AXES, pairs)  29 us
    all_to_all x1, blocking collectives, on_device(): lax.all_to_all(split, ('tm', 'core'), split_axis=0, concat_axis=0, tiled=...  14.4 us
    all_to_all x1, blocking collectives, on_device(): lax.all_to_all(jnp.broadcast_to(control, (SLICES, SEGMENTS)), 'tm', split...  14.3 us
    unnamed x45, local copies, waits for them, and re-layouts  2.84 us
  transfers between devices with their start and end apart: 21, of which 11 were waited for; matrix products, arithmetic and copies ran while one was open for 1% of the time, Pallas kernels for 0%

profile of v2, /device:TPU:4, one launch (start us, length us, event | category | flops | bytes accessed | tf_op | source)
XLA Modules:
  0.0 132.5 jit_solution(16731121993212377324)
XLA Ops:
  0.7 1.3 %fusion.12 = (f32[1,2,82,256]{3,2,1,0:T(8,128)S(1)}, f32[1,2,82,256]{3,2,1,0:T(8,128)S(1)}, f32[1,2,82,256]{3,2,1,0:T(8,128)S(1)}) fusion(s32[]{:T(128)S(6)} %select_n.60, f32[2,25,256]{2,1,0:T(8,128)S(1)} %broadcast_in_dim.18, f32[2,256,256]{2,1,0:T(8,128)} %param.10, f32[2,256,256]{2,1,0:T(8,128)} %param.11, f32[2,1,256]{2,1,0:T(1,128)S(1)} %copy.17, ...), kind=kLoop, calls=%fused_computation.41 | loop fusion | flops 377856 | bytes 2130944 | tf_op jit(solution)/shard_map/stack | solution.py:352
  2.5 7.7 %collective-permute-start.1 = (f32[82,256]{1,0:T(8,128)S(1)}, f32[82,256]{1,0:T(8,128)S(1)}, u32[]{:S(2)}, u32[]{:S(2)}) collective-permute-start(f32[82,256]{1,0:T(8,128)S(1)} %fusion.19), channel_id=1, source_target_pairs={{1,3},{2,0},{3,5},{4,2},{5,7},{6,4},{7,9},{8,6},{9,11},{10,8},{11,... | collective-permute-start | bytes 251912 | tf_op jit(solution)/shard_map/ppermute | solution.py:45
  10.2 2.0 %collective-permute-start.2 = (f32[82,256]{1,0:T(8,128)S(1)}, f32[82,256]{1,0:T(8,128)S(1)}, u32[]{:S(2)}, u32[]{:S(2)}) collective-permute-start(f32[82,256]{1,0:T(8,128)S(1)} %fusion.19), channel_id=1, source_target_pairs={{1,2},{2,1},{3,4},{4,3},{5,6},{6,5},{7,8},{8,7},{9,10},{10,9},{11,... | collective-permute-start | bytes 251912 | tf_op jit(solution)/shard_map/ppermute | solution.py:45
  12.3 5.8 %collective-permute-done.2 = f32[82,256]{1,0:T(8,128)S(1)} collective-permute-done((f32[82,256]{1,0:T(8,128)S(1)}, f32[82,256]{1,0:T(8,128)S(1)}, u32[]{:S(2)}, u32[]{:S(2)}) %collective-permute-start.2) | collective-permute-done | bytes 84000 | tf_op jit(solution)/shard_map/ppermute | solution.py:45
  21.5 1.9 %collective-permute-start.4 = (f32[4,2,64,128]{3,2,1,0:T(8,128)S(1)}, f32[4,2,64,128]{3,2,1,0:T(8,128)S(1)}, u32[]{:S(2)}, u32[]{:S(2)}) collective-permute-start(f32[4,2,64,128]{3,2,1,0:T(8,128)S(1)} %fusion.8), channel_id=1, source_target_pairs={{0,2},{2,4},{3,1},{4,6},{5,3},{6,8},{7,5},{8,10},{9,7},{10,12},{11... | collective-permute-start | bytes 786440 | tf_op jit(solution)/shard_map/ppermute | solution.py:45
  23.5 1.9 %collective-permute-start.3 = (f32[4,2,64,128]{3,2,1,0:T(8,128)S(1)}, f32[4,2,64,128]{3,2,1,0:T(8,128)S(1)}, u32[]{:S(2)}, u32[]{:S(2)}) collective-permute-start(f32[4,2,64,128]{3,2,1,0:T(8,128)S(1)} %fusion.9), channel_id=1, source_target_pairs={{0,2},{2,4},{3,1},{4,6},{5,3},{6,8},{7,5},{8,10},{9,7},{10,12},{11... | collective-permute-start | bytes 786440 | tf_op jit(solution)/shard_map/ppermute | solution.py:45
  25.4 6.5 %collective-permute-done.4.refs_3_ = f32[4,2,64,128]{3,2,1,0:T(8,128)S(1)} collective-permute-done((f32[4,2,64,128]{3,2,1,0:T(8,128)S(1)}, f32[4,2,64,128]{3,2,1,0:T(8,128)S(1)}, u32[]{:S(2)}, u32[]{:S(2)}) %collective-permute-start.4) | collective-permute-done | bytes 262176 | tf_op jit(solution)/shard_map/ppermute | solution.py:45
  31.9 1.9 %collective-permute-start.6 = (f32[4,2,64,128]{3,2,1,0:T(8,128)S(1)}, f32[4,2,64,128]{3,2,1,0:T(8,128)S(1)}, u32[]{:S(2)}, u32[]{:S(2)}) collective-permute-start(f32[4,2,64,128]{3,2,1,0:T(8,128)S(1)} %collective-permute-done.4.refs_3_), channel_id=1, source_target_pairs={{0,2},{2,4},{3,1},{4,6},{5,3},{6,8},{7,5},{8,10},{9,7},{10,12},{11... | collective-permute-start | bytes 786440 | tf_op jit(solution)/shard_map/ppermute | solution.py:45
  34.7 1.9 %collective-permute-start.5 = (f32[4,2,64,128]{3,2,1,0:T(8,128)S(1)}, f32[4,2,64,128]{3,2,1,0:T(8,128)S(1)}, u32[]{:S(2)}, u32[]{:S(2)}) collective-permute-start(f32[4,2,64,128]{3,2,1,0:T(8,128)S(1)} %collective-permute-done.3.refs_2_), channel_id=1, source_target_pairs={{0,2},{2,4},{3,1},{4,6},{5,3},{6,8},{7,5},{8,10},{9,7},{10,12},{11... | collective-permute-start | bytes 786440 | tf_op jit(solution)/shard_map/ppermute | solution.py:45
  37.6 1.9 %collective-permute-start.11 = (f32[2,2,48,128]{3,2,1,0:T(8,128)S(1)}, f32[2,2,48,128]{3,2,1,0:T(8,128)S(1)}, u32[]{:S(2)}, u32[]{:S(2)}) collective-permute-start(f32[2,2,48,128]{3,2,1,0:T(8,128)S(1)} %fusion.18), channel_id=1, source_target_pairs={{0,10},{2,12},{4,14},{6,144},{8,146},{10,148},{11,1},{12,150},{13,... | collective-permute-start | bytes 294920 | tf_op jit(solution)/shard_map/ppermute | solution.py:45
  39.5 5.5 %collective-permute-done.6.refs_5_ = f32[4,2,64,128]{3,2,1,0:T(8,128)S(1)} collective-permute-done((f32[4,2,64,128]{3,2,1,0:T(8,128)S(1)}, f32[4,2,64,128]{3,2,1,0:T(8,128)S(1)}, u32[]{:S(2)}, u32[]{:S(2)}) %collective-permute-start.6) | collective-permute-done | bytes 262176 | tf_op jit(solution)/shard_map/ppermute | solution.py:45
  45.0 1.9 %collective-permute-start.8 = (f32[4,2,48,128]{3,2,1,0:T(8,128)S(1)}, f32[4,2,48,128]{3,2,1,0:T(8,128)S(1)}, u32[]{:S(2)}, u32[]{:S(2)}) collective-permute-start(f32[4,2,48,128]{3,2,1,0:T(8,128)S(1)} %slice.119), channel_id=1, source_target_pairs={{0,2},{2,4},{3,1},{4,6},{5,3},{6,8},{7,5},{8,10},{9,7},{10,12},{11... | collective-permute-start | bytes 589832 | tf_op jit(solution)/shard_map/ppermute | solution.py:45
  46.9 1.2 collective-permute-done.5.refs_4_
  48.2 1.9 %collective-permute-start.7 = (f32[4,2,48,128]{3,2,1,0:T(8,128)S(1)}, f32[4,2,48,128]{3,2,1,0:T(8,128)S(1)}, u32[]{:S(2)}, u32[]{:S(2)}) collective-permute-start(f32[4,2,48,128]{3,2,1,0:T(8,128)S(1)} %slice.118), channel_id=1, source_target_pairs={{0,2},{2,4},{3,1},{4,6},{5,3},{6,8},{7,5},{8,10},{9,7},{10,12},{11... | collective-permute-start | bytes 589832 | tf_op jit(solution)/shard_map/ppermute | solution.py:45
  51.7 3.0 %collective-permute-done.8.refs_7_ = f32[4,2,48,128]{3,2,1,0:T(8,128)S(1)} collective-permute-done((f32[4,2,48,128]{3,2,1,0:T(8,128)S(1)}, f32[4,2,48,128]{3,2,1,0:T(8,128)S(1)}, u32[]{:S(2)}, u32[]{:S(2)}) %collective-permute-start.8) | collective-permute-done | bytes 196640 | tf_op jit(solution)/shard_map/ppermute | solution.py:45
  54.6 1.9 %collective-permute-start.10 = (f32[4,2,48,128]{3,2,1,0:T(8,128)S(1)}, f32[4,2,48,128]{3,2,1,0:T(8,128)S(1)}, u32[]{:S(2)}, u32[]{:S(2)}) collective-permute-start(f32[4,2,48,128]{3,2,1,0:T(8,128)S(1)} %collective-permute-done.8.refs_7_), channel_id=1, source_target_pairs={{0,2},{2,4},{3,1},{4,6},{5,3},{6,8},{7,5},{8,10},{9,7},{10,12},{11... | collective-permute-start | bytes 589832 | tf_op jit(solution)/shard_map/ppermute | solution.py:45
  56.6 1.3 collective-permute-done.7.refs_6_
  57.8 1.9 %collective-permute-start.9 = (f32[4,2,48,128]{3,2,1,0:T(8,128)S(1)}, f32[4,2,48,128]{3,2,1,0:T(8,128)S(1)}, u32[]{:S(2)}, u32[]{:S(2)}) collective-permute-start(f32[4,2,48,128]{3,2,1,0:T(8,128)S(1)} %collective-permute-done.7.refs_6_), channel_id=1, source_target_pairs={{0,2},{2,4},{3,1},{4,6},{5,3},{6,8},{7,5},{8,10},{9,7},{10,12},{11... | collective-permute-start | bytes 589832 | tf_op jit(solution)/shard_map/ppermute | solution.py:45
  60.8 3.5 %collective-permute-done.10.refs_9_ = f32[4,2,48,128]{3,2,1,0:T(8,128)S(1)} collective-permute-done((f32[4,2,48,128]{3,2,1,0:T(8,128)S(1)}, f32[4,2,48,128]{3,2,1,0:T(8,128)S(1)}, u32[]{:S(2)}, u32[]{:S(2)}) %collective-permute-start.10) | collective-permute-done | bytes 196640 | tf_op jit(solution)/shard_map/ppermute | solution.py:45
  64.3 3.2 %collective-permute-done.9.refs_8_ = f32[4,2,48,128]{3,2,1,0:T(8,128)S(1)} collective-permute-done((f32[4,2,48,128]{3,2,1,0:T(8,128)S(1)}, f32[4,2,48,128]{3,2,1,0:T(8,128)S(1)}, u32[]{:S(2)}, u32[]{:S(2)}) %collective-permute-start.9) | collective-permute-done | bytes 196640 | tf_op jit(solution)/shard_map/ppermute | solution.py:45
  67.5 14.3 %all_to_all.13 = f32[8,1,16]{2,1,0:T(1,128)} all-to-all(f32[8,1,16]{2,1,0:T(1,128)S(1)} %broadcast_in_dim.17), channel_id=1, replica_groups=mesh['tm'=8,'chip'=16,'core'=2] {'tm'}, dimensions={0} | all-to-all | bytes 1024 | tf_op jit(solution)/shard_map/all_to_all | solution.py:344
  82.9 33.4 %parareal.1 = f32[8,4,16,256]{3,2,1,0:T(8,128)} custom-call(f32[8,16]{1,0:T(8,128)} %bitcast.57, f32[4,2,80,128]{3,2,1,0:T(8,128)} %get-tuple-element.26.refs_0_, f32[4,2,80,128]{3,2,1,0:T(8,128)} %get-tuple-element.20.refs_1_, f32[4,2,64,128]{3,2,1,0:T(8,128)} %copy-done.6, f32[4,2,64,128]{3,2,1,0:T(8,128)} %copy-done.5, f32[4,2,64,128]{3,2,1,0:T(8,128)} %copy-done.2, ...), custom_call_target="tpu_custom_call" | custom-call | tf_op jit(solution)/shard_map/parareal/pallas_call | solution.py:324
  116.2 14.4 %all_to_all.14 = f32[16,2,16,256]{3,2,1,0:T(8,128)S(1)} all-to-all(f32[16,2,16,256]{3,2,1,0:T(8,128)} %bitcast.55), channel_id=1, replica_groups=mesh['tm'=8,'chip'=16,'core'=2] {'tm','core'}, dimensions={0} | all-to-all | bytes 1048576 | tf_op jit(solution)/shard_map/all_to_all | solution.py:385
  130.7 0.9 copy-done
  (92 shorter events, 10.7 us)
Async XLA Ops:
  2.4 15.8 %collective-permute-start = (f32[3,2,82,256]{3,1,2,0:T(2,128)S(1)}, f32[3,2,82,256]{3,1,2,0:T(2,128)S(1)}, u32[]{:S(2)}, u32[]{:S(2)}) collective-permute-start(f32[3,2,82,256]{3,1,2,0:T(2,128)S(1)} %copy.12), channel_id=1, source_target_pairs={{0,1},{1,0},{2,3},{3,2},{4,5},{5,4},{6,7},{7,6},{8,9},{9,8},{10,11... | collective-permute-start | bytes 1511432 | tf_op jit(solution)/shard_map/ppermute | solution.py:45
  2.5 9.9 %collective-permute-start.1 = (f32[82,256]{1,0:T(8,128)S(1)}, f32[82,256]{1,0:T(8,128)S(1)}, u32[]{:S(2)}, u32[]{:S(2)}) collective-permute-start(f32[82,256]{1,0:T(8,128)S(1)} %fusion.19), channel_id=1, source_target_pairs={{1,3},{2,0},{3,5},{4,2},{5,7},{6,4},{7,9},{8,6},{9,11},{10,8},{11,... | collective-permute-start | bytes 251912 | tf_op jit(solution)/shard_map/ppermute | solution.py:45
  10.2 8.0 %collective-permute-start.2 = (f32[82,256]{1,0:T(8,128)S(1)}, f32[82,256]{1,0:T(8,128)S(1)}, u32[]{:S(2)}, u32[]{:S(2)}) collective-permute-start(f32[82,256]{1,0:T(8,128)S(1)} %fusion.19), channel_id=1, source_target_pairs={{1,2},{2,1},{3,4},{4,3},{5,6},{6,5},{7,8},{8,7},{9,10},{10,9},{11,... | collective-permute-start | bytes 251912 | tf_op jit(solution)/shard_map/ppermute | solution.py:45
  21.5 10.4 %collective-permute-start.4 = (f32[4,2,64,128]{3,2,1,0:T(8,128)S(1)}, f32[4,2,64,128]{3,2,1,0:T(8,128)S(1)}, u32[]{:S(2)}, u32[]{:S(2)}) collective-permute-start(f32[4,2,64,128]{3,2,1,0:T(8,128)S(1)} %fusion.8), channel_id=1, source_target_pairs={{0,2},{2,4},{3,1},{4,6},{5,3},{6,8},{7,5},{8,10},{9,7},{10,12},{11... | collective-permute-start | bytes 786440 | tf_op jit(solution)/shard_map/ppermute | solution.py:45
  23.5 11.2 %collective-permute-start.3 = (f32[4,2,64,128]{3,2,1,0:T(8,128)S(1)}, f32[4,2,64,128]{3,2,1,0:T(8,128)S(1)}, u32[]{:S(2)}, u32[]{:S(2)}) collective-permute-start(f32[4,2,64,128]{3,2,1,0:T(8,128)S(1)} %fusion.9), channel_id=1, source_target_pairs={{0,2},{2,4},{3,1},{4,6},{5,3},{6,8},{7,5},{8,10},{9,7},{10,12},{11... | collective-permute-start | bytes 786440 | tf_op jit(solution)/shard_map/ppermute | solution.py:45
  31.9 13.1 %collective-permute-start.6 = (f32[4,2,64,128]{3,2,1,0:T(8,128)S(1)}, f32[4,2,64,128]{3,2,1,0:T(8,128)S(1)}, u32[]{:S(2)}, u32[]{:S(2)}) collective-permute-start(f32[4,2,64,128]{3,2,1,0:T(8,128)S(1)} %collective-permute-done.4.refs_3_), channel_id=1, source_target_pairs={{0,2},{2,4},{3,1},{4,6},{5,3},{6,8},{7,5},{8,10},{9,7},{10,12},{11... | collective-permute-start | bytes 786440 | tf_op jit(solution)/shard_map/ppermute | solution.py:45
  34.7 13.4 %collective-permute-start.5 = (f32[4,2,64,128]{3,2,1,0:T(8,128)S(1)}, f32[4,2,64,128]{3,2,1,0:T(8,128)S(1)}, u32[]{:S(2)}, u32[]{:S(2)}) collective-permute-start(f32[4,2,64,128]{3,2,1,0:T(8,128)S(1)} %collective-permute-done.3.refs_2_), channel_id=1, source_target_pairs={{0,2},{2,4},{3,1},{4,6},{5,3},{6,8},{7,5},{8,10},{9,7},{10,12},{11... | collective-permute-start | bytes 786440 | tf_op jit(solution)/shard_map/ppermute | solution.py:45
  37.6 12.5 %collective-permute-start.11 = (f32[2,2,48,128]{3,2,1,0:T(8,128)S(1)}, f32[2,2,48,128]{3,2,1,0:T(8,128)S(1)}, u32[]{:S(2)}, u32[]{:S(2)}) collective-permute-start(f32[2,2,48,128]{3,2,1,0:T(8,128)S(1)} %fusion.18), channel_id=1, source_target_pairs={{0,10},{2,12},{4,14},{6,144},{8,146},{10,148},{11,1},{12,150},{13,... | collective-permute-start | bytes 294920 | tf_op jit(solution)/shard_map/ppermute | solution.py:45
  45.0 37.0 %copy-start.1 = (f32[4,2,64,128]{3,2,1,0:T(8,128)}, f32[4,2,64,128]{3,2,1,0:T(8,128)S(1)}, u32[]{:S(2)}) copy-start(f32[4,2,64,128]{3,2,1,0:T(8,128)S(1)} %collective-permute-done.6.refs_5_) | copy-start | bytes 786436
  45.0 9.7 %collective-permute-start.8 = (f32[4,2,48,128]{3,2,1,0:T(8,128)S(1)}, f32[4,2,48,128]{3,2,1,0:T(8,128)S(1)}, u32[]{:S(2)}, u32[]{:S(2)}) collective-permute-start(f32[4,2,48,128]{3,2,1,0:T(8,128)S(1)} %slice.119), channel_id=1, source_target_pairs={{0,2},{2,4},{3,1},{4,6},{5,3},{6,8},{7,5},{8,10},{9,7},{10,12},{11... | collective-permute-start | bytes 589832 | tf_op jit(solution)/shard_map/ppermute | solution.py:45
  48.1 33.8 %copy-start.2 = (f32[4,2,64,128]{3,2,1,0:T(8,128)}, f32[4,2,64,128]{3,2,1,0:T(8,128)S(1)}, u32[]{:S(2)}) copy-start(f32[4,2,64,128]{3,2,1,0:T(8,128)S(1)} %collective-permute-done.5.refs_4_) | copy-start | bytes 786436
  48.2 9.7 %collective-permute-start.7 = (f32[4,2,48,128]{3,2,1,0:T(8,128)S(1)}, f32[4,2,48,128]{3,2,1,0:T(8,128)S(1)}, u32[]{:S(2)}, u32[]{:S(2)}) collective-permute-start(f32[4,2,48,128]{3,2,1,0:T(8,128)S(1)} %slice.118), channel_id=1, source_target_pairs={{0,2},{2,4},{3,1},{4,6},{5,3},{6,8},{7,5},{8,10},{9,7},{10,12},{11... | collective-permute-start | bytes 589832 | tf_op jit(solution)/shard_map/ppermute | solution.py:45
  50.1 31.9 %copy-start.19 = (f32[2,2,48,128]{3,2,1,0:T(8,128)}, f32[2,2,48,128]{3,2,1,0:T(8,128)S(1)}, u32[]{:S(2)}) copy-start(f32[2,2,48,128]{3,2,1,0:T(8,128)S(1)} %collective-permute-done.11.refs_10_) | copy-start | bytes 294916
  50.1 1.4 %collective-permute-start.20 = (f32[2,2,48,128]{3,2,1,0:T(8,128)S(1)}, f32[2,2,48,128]{3,2,1,0:T(8,128)S(1)}, u32[]{:S(2)}, u32[]{:S(2)}) collective-permute-start(f32[2,2,48,128]{3,2,1,0:T(8,128)S(1)} %collective-permute-done.11.refs_10_), channel_id=1, source_target_pairs={{0,1},{1,0},{2,3},{3,2},{4,5},{5,4},{6,7},{7,6},{8,9},{9,8},{10,11... | collective-permute-start | bytes 294920 | tf_op jit(solution)/shard_map/ppermute | solution.py:45
  50.2 9.5 %collective-permute-start.13 = (f32[4,2,64,128]{3,2,1,0:T(8,128)S(1)}, f32[4,2,64,128]{3,2,1,0:T(8,128)S(1)}, u32[]{:S(2)}, u32[]{:S(2)}) collective-permute-start(f32[4,2,64,128]{3,2,1,0:T(8,128)S(1)} %collective-permute-done.4.refs_3_), channel_id=1, source_target_pairs={{0,1},{1,0},{2,3},{3,2},{4,5},{5,4},{6,7},{7,6},{8,9},{9,8},{10,11... | collective-permute-start | bytes 786440 | tf_op jit(solution)/shard_map/ppermute | solution.py:45
  50.7 9.6 %collective-permute-start.12 = (f32[4,2,64,128]{3,2,1,0:T(8,128)S(1)}, f32[4,2,64,128]{3,2,1,0:T(8,128)S(1)}, u32[]{:S(2)}, u32[]{:S(2)}) collective-permute-start(f32[4,2,64,128]{3,2,1,0:T(8,128)S(1)} %collective-permute-done.3.refs_2_), channel_id=1, source_target_pairs={{0,1},{1,0},{2,3},{3,2},{4,5},{5,4},{6,7},{7,6},{8,9},{9,8},{10,11... | collective-permute-start | bytes 786440 | tf_op jit(solution)/shard_map/ppermute | solution.py:45
  51.5 9.0 %collective-permute-start.15 = (f32[4,2,64,128]{3,2,1,0:T(8,128)S(1)}, f32[4,2,64,128]{3,2,1,0:T(8,128)S(1)}, u32[]{:S(2)}, u32[]{:S(2)}) collective-permute-start(f32[4,2,64,128]{3,2,1,0:T(8,128)S(1)} %collective-permute-done.6.refs_5_), channel_id=1, source_target_pairs={{0,1},{1,0},{2,3},{3,2},{4,5},{5,4},{6,7},{7,6},{8,9},{9,8},{10,11... | collective-permute-start | bytes 786440 | tf_op jit(solution)/shard_map/ppermute | solution.py:45
  54.6 9.7 %collective-permute-start.10 = (f32[4,2,48,128]{3,2,1,0:T(8,128)S(1)}, f32[4,2,48,128]{3,2,1,0:T(8,128)S(1)}, u32[]{:S(2)}, u32[]{:S(2)}) collective-permute-start(f32[4,2,48,128]{3,2,1,0:T(8,128)S(1)} %collective-permute-done.8.refs_7_), channel_id=1, source_target_pairs={{0,2},{2,4},{3,1},{4,6},{5,3},{6,8},{7,5},{8,10},{9,7},{10,12},{11... | collective-permute-start | bytes 589832 | tf_op jit(solution)/shard_map/ppermute | solution.py:45
  57.8 9.7 %collective-permute-start.9 = (f32[4,2,48,128]{3,2,1,0:T(8,128)S(1)}, f32[4,2,48,128]{3,2,1,0:T(8,128)S(1)}, u32[]{:S(2)}, u32[]{:S(2)}) collective-permute-start(f32[4,2,48,128]{3,2,1,0:T(8,128)S(1)} %collective-permute-done.7.refs_6_), channel_id=1, source_target_pairs={{0,2},{2,4},{3,1},{4,6},{5,3},{6,8},{7,5},{8,10},{9,7},{10,12},{11... | collective-permute-start | bytes 589832 | tf_op jit(solution)/shard_map/ppermute | solution.py:45
  59.8 22.1 %collective-permute-start.14 = (f32[4,2,64,128]{3,2,1,0:T(8,128)S(1)}, f32[4,2,64,128]{3,2,1,0:T(8,128)S(1)}, u32[]{:S(2)}, u32[]{:S(2)}) collective-permute-start(f32[4,2,64,128]{3,2,1,0:T(8,128)S(1)} %collective-permute-done.5.refs_4_), channel_id=1, source_target_pairs={{0,1},{1,0},{2,3},{3,2},{4,5},{5,4},{6,7},{7,6},{8,9},{9,8},{10,11... | collective-permute-start | bytes 786440 | tf_op jit(solution)/shard_map/ppermute | solution.py:45
  60.3 21.5 %collective-permute-start.17 = (f32[4,2,48,128]{3,2,1,0:T(8,128)S(1)}, f32[4,2,48,128]{3,2,1,0:T(8,128)S(1)}, u32[]{:S(2)}, u32[]{:S(2)}) collective-permute-start(f32[4,2,48,128]{3,2,1,0:T(8,128)S(1)} %collective-permute-done.8.refs_7_), channel_id=1, source_target_pairs={{0,1},{1,0},{2,3},{3,2},{4,5},{5,4},{6,7},{7,6},{8,9},{9,8},{10,11... | collective-permute-start | bytes 589832 | tf_op jit(solution)/shard_map/ppermute | solution.py:45
  60.5 21.4 %collective-permute-start.16 = (f32[4,2,48,128]{3,2,1,0:T(8,128)S(1)}, f32[4,2,48,128]{3,2,1,0:T(8,128)S(1)}, u32[]{:S(2)}, u32[]{:S(2)}) collective-permute-start(f32[4,2,48,128]{3,2,1,0:T(8,128)S(1)} %collective-permute-done.7.refs_6_), channel_id=1, source_target_pairs={{0,1},{1,0},{2,3},{3,2},{4,5},{5,4},{6,7},{7,6},{8,9},{9,8},{10,11... | collective-permute-start | bytes 589832 | tf_op jit(solution)/shard_map/ppermute | solution.py:45
  64.3 17.6 %collective-permute-start.19 = (f32[4,2,48,128]{3,2,1,0:T(8,128)S(1)}, f32[4,2,48,128]{3,2,1,0:T(8,128)S(1)}, u32[]{:S(2)}, u32[]{:S(2)}) collective-permute-start(f32[4,2,48,128]{3,2,1,0:T(8,128)S(1)} %collective-permute-done.10.refs_9_), channel_id=1, source_target_pairs={{0,1},{1,0},{2,3},{3,2},{4,5},{5,4},{6,7},{7,6},{8,9},{9,8},{10,11... | collective-permute-start | bytes 589832 | tf_op jit(solution)/shard_map/ppermute | solution.py:45
  67.5 14.4 %collective-permute-start.18 = (f32[4,2,48,128]{3,2,1,0:T(8,128)S(1)}, f32[4,2,48,128]{3,2,1,0:T(8,128)S(1)}, u32[]{:S(2)}, u32[]{:S(2)}) collective-permute-start(f32[4,2,48,128]{3,2,1,0:T(8,128)S(1)} %collective-permute-done.9.refs_8_), channel_id=1, source_target_pairs={{0,1},{1,0},{2,3},{3,2},{4,5},{5,4},{6,7},{7,6},{8,9},{9,8},{10,11... | collective-permute-start | bytes 589832 | tf_op jit(solution)/shard_map/ppermute | solution.py:45
  (19 other events, 250.9 us)

commit v3 on v2

--- a/solution.py
+++ b/solution.py
@@ -341,7 +341,13 @@
 def on_device(initial_state, capacity, source, control, segment_index):
     tm, chip, core = lax.axis_index("tm"), lax.axis_index("chip"), lax.axis_index("core")
     block = jnp.where(chip >= CHIPS // 2, tm ^ 4, tm)
-    controls = lax.all_to_all(jnp.broadcast_to(control, (SLICES, SEGMENTS)), "tm", split_axis=0, concat_axis=0, tiled=True)
+    rows = lax.broadcasted_iota(jnp.int32, (SLICES, 1), 0)
+    controls = jnp.where(rows == tm, control, 0.0)
+
+    def spread(controls, bit):
+        return controls + lax.ppermute(controls, "tm", [(t, t ^ bit) for t in range(SLICES)])
+
+    first = spread(controls, 1)
 
     above = jnp.zeros((2, 25, 256), jnp.float32)
     marked = above.at[:, 17, :].set(segment_index.astype(jnp.float32))
@@ -349,35 +355,47 @@
     def window(x, top):
         return lax.dynamic_slice_in_dim(jnp.concatenate([top, x, above], axis=1), 32 * block, 82, axis=1)
 
-    mine = jnp.stack([window(capacity, above), window(source, marked), window(initial_state, above)])
-    theirs = send(mine, PARTNER)
-    outer = jnp.where(core == 0, mine[2, 0], mine[2, 1])
+    def beside(x):
+        y = send(x, PARTNER)
+        return jnp.where(core == 0, jnp.concatenate([x, y], axis=-3), jnp.concatenate([y, x], axis=-3))
+
+    chip_c = beside(window(capacity, above))
+    mine = jnp.stack([window(source, marked), window(initial_state, above)])
+    outer = jnp.where(core == 0, mine[1, 0], mine[1, 1])
     facing = send(outer, FACING)
     facing_same = send(outer, FACING_SAME)
-    chip4 = jnp.where(core == 0, jnp.concatenate([mine, theirs], axis=1), jnp.concatenate([theirs, mine], axis=1))
+    chip4 = beside(mine)
     before = jnp.where(core == 0, facing, facing_same)
     after = jnp.where(core == 0, facing_same, facing)
-    state = jnp.concatenate([before[None], chip4[2], after[None]], axis=0)
+    state = jnp.concatenate([before[None], chip4[1], after[None]], axis=0)
     middle = state[1:-1, 1:-1]
     deeper = jnp.pad(middle, ((0, 0), (0, 0), (1, 1)))
     residual = (state[2:, 1:-1] + state[:-2, 1:-1] + state[1:-1, 2:] + state[1:-1, :-2]
-                + deeper[:, :, 2:] + deeper[:, :, :-2] - 6.0 * middle + chip4[1, :, 1:-1])
+                + deeper[:, :, 2:] + deeper[:, :, :-2] - 6.0 * middle + chip4[0, :, 1:-1])
     order = jnp.asarray(lane_order())
 
     def laid(x):
         return jnp.stack([jnp.dot(x, order[:, h * LANES:(h + 1) * LANES], precision=lax.Precision.HIGHEST)
                           for h in range(2)], axis=1)
 
-    own_c, own_q = laid(chip4[0, :, 1:-1]), laid(residual)
+    own_c, own_q = laid(chip_c[:, 1:-1]), laid(residual)
     x_c, x_q = own_c[:, :, 8:72], own_q[:, :, 8:72]
     got = []
+    edge = jnp.stack([own_c, own_q])[:, :, :, 16:64]
+    edge = jnp.where(core == 0, edge[:, 3], edge[:, 0])
     for k in range(4):
         if k == 2:
             x_c, x_q = x_c[:, :, 8:56], x_q[:, :, 8:56]
         x_c, x_q = send(x_c, OUTWARD), send(x_q, OUTWARD)
         got += [x_c, x_q]
-    edge = jnp.stack([own_c, own_q])[:, :, :, 16:64]
-    got.append(send(jnp.where(core == 0, edge[:, 3], edge[:, 0]), OUTWARD_5))
+        if k == 0:
+            first, x_c = lax.optimization_barrier((first, x_c))
+            second = spread(first, 2)
+        if k == 1:
+            edge, second, x_c = lax.optimization_barrier((edge, second, x_c))
+            end_cq = send(edge, OUTWARD_5)
+            controls = spread(second, 4)
+    got.append(end_cq)
     passed = [send(x, PARTNER) for x in got]
     ends = solve(controls, own_c, own_q, *got, *passed)
 

time: 133 us -> 121 us (0.910)
  waiting for transfers between devices: 31.6 us -> 18.1 us
  starting transfers between devices: 29 us -> 42.2 us
  blocking collectives: 28.7 us -> 16.5 us
    ppermute x21 -> x22, waiting for transfers between devices: 31.6 us -> 12.6 us  [send(): return lax.ppermute(x, AXES, pairs)]
    all_to_all x1 -> x0, blocking collectives: 14.3 us -> none  [on_device(): lax.all_to_all(jnp.broadcast_to(control, (SLICES, SEGMENTS)), 'tm', split...]
    ppermute x0 -> x3, starting transfers between devices: none -> 7.5 us  [spread(): lax.ppermute(controls, 'tm', [(t, t ^ bit) for t in range(SLICES)])]
    ppermute x21 -> x22, starting transfers between devices: 29 us -> 34.7 us  [send(): return lax.ppermute(x, AXES, pairs)]
    ppermute x0 -> x3, waiting for transfers between devices: none -> 5.53 us  [spread(): lax.ppermute(controls, 'tm', [(t, t ^ bit) for t in range(SLICES)])]
    another operation x4 -> x2, other arithmetic: 3 us -> 0.03 us  [the longest x1 0.03 us: on_device(): mine = jnp.stack([window(source, marked), window(initial_state, above)])]
    all_to_all x1, blocking collectives: 14.4 us -> 16.5 us  [on_device(): lax.all_to_all(split, ('tm', 'core'), split_axis=0, concat_axis=0, tiled=...]
    another operation x2 -> x4, other arithmetic: 0.04 us -> 1.57 us  [laid(): jnp.stack([jnp.dot(x, order[:, h * LANES:(h + 1) * LANES], precision=lax....]
  transfers between devices with their start and end apart: 21 -> 25, of which waited for: 11 -> 10; matrix products, arithmetic and copies ran while one was open for 1% -> 4% of each run, Pallas kernels for 0% -> 0%
where the time goes in v3:
time: 121 us; the launch traced here: 120 us
  starting transfers between devices  42.2 us (35%)
  Pallas kernels  33.2 us (27%)
  waiting for transfers between devices  18.1 us (15%)
  blocking collectives  16.5 us (14%)
  other arithmetic  5 us (4%)
  local copies, waits for them, and re-layouts  2.86 us (2%)
  matrix products  1.75 us (1%)
    ppermute x22, starting transfers between devices, send(): return lax.ppermute(x, AXES, pairs)  34.7 us
    pallas_call x1, Pallas kernels, solve(): pl.pallas_call(main_kernel, out_shape=jax.ShapeDtypeStruct((SLICES, 4, 16...  33.2 us
    all_to_all x1, blocking collectives, on_device(): lax.all_to_all(split, ('tm', 'core'), split_axis=0, concat_axis=0, tiled=...  16.5 us
    ppermute x22, waiting for transfers between devices, send(): return lax.ppermute(x, AXES, pairs)  12.6 us
    ppermute x3, starting transfers between devices, spread(): lax.ppermute(controls, 'tm', [(t, t ^ bit) for t in range(SLICES)])  7.5 us
    ppermute x3, waiting for transfers between devices, spread(): lax.ppermute(controls, 'tm', [(t, t ^ bit) for t in range(SLICES)])  5.53 us
    unnamed x47, local copies, waits for them, and re-layouts  2.74 us
  transfers between devices with their start and end apart: 25, of which 10 were waited for; matrix products, arithmetic and copies ran while one was open for 4% of the time, Pallas kernels for 0%

profile of v3, /device:TPU:4, one launch (start us, length us, event | category | flops | bytes accessed | tf_op | source)
XLA Modules:
  0.0 120.1 jit_solution(4822982589879552217)
XLA Ops:
  0.7 1.3 %fusion.8 = (f32[2,82,256]{2,1,0:T(8,128)S(1)}, f32[1,2,82,256]{3,2,1,0:T(8,128)S(1)}, f32[1,2,82,256]{3,2,1,0:T(8,128)S(1)}) fusion(s32[]{:T(128)S(6)} %select_n.73, f32[2,25,256]{2,1,0:T(8,128)S(1)} %broadcast_in_dim.34, f32[2,256,256]{2,1,0:T(8,128)} %param.10, f32[2,256,256]{2,1,0:T(8,128)} %param.11, f32[2,1,256]{2,1,0:T(1,128)S(1)} %copy.11, ...), kind=kLoop, calls=%fused_computation.38 | loop fusion | flops 377856 | bytes 2130944 | tf_op jit(solution)/shard_map/concatenate | solution.py:356
  2.1 7.2 %collective-permute-start.3 = (f32[82,256]{1,0:T(8,128)S(1)}, f32[82,256]{1,0:T(8,128)S(1)}, u32[]{:S(2)}, u32[]{:S(2)}) collective-permute-start(f32[82,256]{1,0:T(8,128)S(1)} %fusion.23), channel_id=1, source_target_pairs={{1,2},{2,1},{3,4},{4,3},{5,6},{6,5},{7,8},{8,7},{9,10},{10,9},{11,... | collective-permute-start | bytes 251912 | tf_op jit(solution)/shard_map/ppermute | solution.py:45
  9.3 2.9 %collective-permute-start.2 = (f32[82,256]{1,0:T(8,128)S(1)}, f32[82,256]{1,0:T(8,128)S(1)}, u32[]{:S(2)}, u32[]{:S(2)}) collective-permute-start(f32[82,256]{1,0:T(8,128)S(1)} %fusion.23), channel_id=1, source_target_pairs={{1,3},{2,0},{3,5},{4,2},{5,7},{6,4},{7,9},{8,6},{9,11},{10,8},{11,... | collective-permute-start | bytes 251912 | tf_op jit(solution)/shard_map/ppermute | solution.py:45
  12.9 2.8 %collective-permute-done.2 = f32[82,256]{1,0:T(8,128)S(1)} collective-permute-done((f32[82,256]{1,0:T(8,128)S(1)}, f32[82,256]{1,0:T(8,128)S(1)}, u32[]{:S(2)}, u32[]{:S(2)}) %collective-permute-start.2) | collective-permute-done | bytes 84000 | tf_op jit(solution)/shard_map/ppermute | solution.py:45
  17.1 1.9 %collective-permute-start.5 = (f32[4,2,64,128]{3,2,1,0:T(8,128)S(1)}, f32[4,2,64,128]{3,2,1,0:T(8,128)S(1)}, u32[]{:S(2)}, u32[]{:S(2)}) collective-permute-start(f32[4,2,64,128]{3,2,1,0:T(8,128)S(1)} %fusion.10), channel_id=1, source_target_pairs={{0,2},{2,4},{3,1},{4,6},{5,3},{6,8},{7,5},{8,10},{9,7},{10,12},{11... | collective-permute-start | bytes 786440 | tf_op jit(solution)/shard_map/ppermute | solution.py:45
  20.3 1.9 %collective-permute-start.9 = (f32[4,2,64,128]{3,2,1,0:T(8,128)S(1)}, f32[4,2,64,128]{3,2,1,0:T(8,128)S(1)}, u32[]{:S(2)}, u32[]{:S(2)}) collective-permute-start(f32[4,2,64,128]{3,2,1,0:T(8,128)S(1)} %fusion.9), channel_id=1, source_target_pairs={{0,2},{2,4},{3,1},{4,6},{5,3},{6,8},{7,5},{8,10},{9,7},{10,12},{11... | collective-permute-start | bytes 786440 | tf_op jit(solution)/shard_map/ppermute | solution.py:45
  22.4 1.6 %collective-permute-start.4 = (f32[8,16]{1,0:T(8,128)S(1)}, f32[8,16]{1,0:T(8,128)S(1)}, u32[]{:S(2)}, u32[]{:S(2)}) collective-permute-start(f32[8,16]{1,0:T(8,128)S(1)} %broadcast_select_fusion), channel_id=1, source_target_pairs={{0,32},{32,0},{64,96},{96,64},{128,160},{160,128},{192,224},{224,1... | collective-permute-start | bytes 1544 | tf_op jit(solution)/shard_map/ppermute | solution.py:348
  24.0 2.0 %collective-permute-done.4 = f32[8,16]{1,0:T(8,128)S(1)} collective-permute-done((f32[8,16]{1,0:T(8,128)S(1)}, f32[8,16]{1,0:T(8,128)S(1)}, u32[]{:S(2)}, u32[]{:S(2)}) %collective-permute-start.4) | collective-permute-done | bytes 544 | tf_op jit(solution)/shard_map/ppermute | solution.py:348
  26.1 1.4 %collective-permute-done.5.refs_2_ = f32[4,2,64,128]{3,2,1,0:T(8,128)S(1)} collective-permute-done((f32[4,2,64,128]{3,2,1,0:T(8,128)S(1)}, f32[4,2,64,128]{3,2,1,0:T(8,128)S(1)}, u32[]{:S(2)}, u32[]{:S(2)}) %collective-permute-start.5) | collective-permute-done | bytes 262176 | tf_op jit(solution)/shard_map/ppermute | solution.py:45
  27.5 2.2 %collective-permute-start.7 = (f32[4,2,64,128]{3,2,1,0:T(8,128)S(1)}, f32[4,2,64,128]{3,2,1,0:T(8,128)S(1)}, u32[]{:S(2)}, u32[]{:S(2)}) collective-permute-start(f32[4,2,64,128]{3,2,1,0:T(8,128)S(1)} %collective-permute-done.5.refs_2_), channel_id=1, source_target_pairs={{0,2},{2,4},{3,1},{4,6},{5,3},{6,8},{7,5},{8,10},{9,7},{10,12},{11... | collective-permute-start | bytes 786440 | tf_op jit(solution)/shard_map/ppermute | solution.py:45
  30.7 2.8 %collective-permute-start.10 = (f32[4,2,64,128]{3,2,1,0:T(8,128)S(1)}, f32[4,2,64,128]{3,2,1,0:T(8,128)S(1)}, u32[]{:S(2)}, u32[]{:S(2)}) collective-permute-start(f32[4,2,64,128]{3,2,1,0:T(8,128)S(1)} %collective-permute-done.9.refs_3_), channel_id=1, source_target_pairs={{0,2},{2,4},{3,1},{4,6},{5,3},{6,8},{7,5},{8,10},{9,7},{10,12},{11... | collective-permute-start | bytes 786440 | tf_op jit(solution)/shard_map/ppermute | solution.py:45
  35.0 3.2 %collective-permute-start.6 = (f32[8,16]{1,0:T(8,128)S(1)}, f32[8,16]{1,0:T(8,128)S(1)}, u32[]{:S(2)}, u32[]{:S(2)}) collective-permute-start(f32[8,16]{1,0:T(8,128)S(1)} %fusion.24), channel_id=1, source_target_pairs={{0,64},{32,96},{64,0},{96,32},{128,192},{160,224},{192,128},{224,1... | collective-permute-start | bytes 1544 | tf_op jit(solution)/shard_map/ppermute | solution.py:348
  38.2 1.9 %collective-permute-done.6 = f32[8,16]{1,0:T(8,128)S(1)} collective-permute-done((f32[8,16]{1,0:T(8,128)S(1)}, f32[8,16]{1,0:T(8,128)S(1)}, u32[]{:S(2)}, u32[]{:S(2)}) %collective-permute-start.6) | collective-permute-done | bytes 544 | tf_op jit(solution)/shard_map/ppermute | solution.py:348
  40.2 3.4 %collective-permute-start.11 = (f32[4,2,48,128]{3,2,1,0:T(8,128)S(1)}, f32[4,2,48,128]{3,2,1,0:T(8,128)S(1)}, u32[]{:S(2)}, u32[]{:S(2)}) collective-permute-start(f32[4,2,48,128]{3,2,1,0:T(8,128)S(1)} %slice.104), channel_id=1, source_target_pairs={{0,2},{2,4},{3,1},{4,6},{5,3},{6,8},{7,5},{8,10},{9,7},{10,12},{11... | collective-permute-start | bytes 589832 | tf_op jit(solution)/shard_map/ppermute | solution.py:45
  43.6 2.9 %collective-permute-start.12 = (f32[4,2,48,128]{3,2,1,0:T(8,128)S(1)}, f32[4,2,48,128]{3,2,1,0:T(8,128)S(1)}, u32[]{:S(2)}, u32[]{:S(2)}) collective-permute-start(f32[4,2,48,128]{3,2,1,0:T(8,128)S(1)} %slice.117), channel_id=1, source_target_pairs={{0,2},{2,4},{3,1},{4,6},{5,3},{6,8},{7,5},{8,10},{9,7},{10,12},{11... | collective-permute-start | bytes 589832 | tf_op jit(solution)/shard_map/ppermute | solution.py:45
  47.2 2.7 %collective-permute-start.8 = (f32[8,16]{1,0:T(8,128)S(1)}, f32[8,16]{1,0:T(8,128)S(1)}, u32[]{:S(2)}, u32[]{:S(2)}) collective-permute-start(f32[8,16]{1,0:T(8,128)S(1)} %add.49), channel_id=1, source_target_pairs={{0,128},{32,160},{64,192},{96,224},{128,0},{160,32},{192,64},{224,... | collective-permute-start | bytes 1544 | tf_op jit(solution)/shard_map/ppermute | solution.py:348
  49.9 1.6 %collective-permute-done.8 = f32[8,16]{1,0:T(8,128)S(1)} collective-permute-done((f32[8,16]{1,0:T(8,128)S(1)}, f32[8,16]{1,0:T(8,128)S(1)}, u32[]{:S(2)}, u32[]{:S(2)}) %collective-permute-start.8) | collective-permute-done | bytes 544 | tf_op jit(solution)/shard_map/ppermute | solution.py:348
  51.5 1.9 %collective-permute-start.15 = (f32[2,2,48,128]{3,2,1,0:T(8,128)S(1)}, f32[2,2,48,128]{3,2,1,0:T(8,128)S(1)}, u32[]{:S(2)}, u32[]{:S(2)}) collective-permute-start(f32[2,2,48,128]{3,2,1,0:T(8,128)S(1)} %fusion.22), channel_id=1, source_target_pairs={{0,10},{2,12},{4,14},{6,144},{8,146},{10,148},{11,1},{12,150},{13,... | collective-permute-start | bytes 294920 | tf_op jit(solution)/shard_map/ppermute | solution.py:45
  53.4 3.2 %collective-permute-start.13 = (f32[4,2,48,128]{3,2,1,0:T(8,128)S(1)}, f32[4,2,48,128]{3,2,1,0:T(8,128)S(1)}, u32[]{:S(2)}, u32[]{:S(2)}) collective-permute-start(f32[4,2,48,128]{3,2,1,0:T(8,128)S(1)} %collective-permute-done.11.refs_6_), channel_id=1, source_target_pairs={{0,2},{2,4},{3,1},{4,6},{5,3},{6,8},{7,5},{8,10},{9,7},{10,12},{11... | collective-permute-start | bytes 589832 | tf_op jit(solution)/shard_map/ppermute | solution.py:45
  56.7 1.9 %collective-permute-start.14 = (f32[4,2,48,128]{3,2,1,0:T(8,128)S(1)}, f32[4,2,48,128]{3,2,1,0:T(8,128)S(1)}, u32[]{:S(2)}, u32[]{:S(2)}) collective-permute-start(f32[4,2,48,128]{3,2,1,0:T(8,128)S(1)} %collective-permute-done.12.refs_7_), channel_id=1, source_target_pairs={{0,2},{2,4},{3,1},{4,6},{5,3},{6,8},{7,5},{8,10},{9,7},{10,12},{11... | collective-permute-start | bytes 589832 | tf_op jit(solution)/shard_map/ppermute | solution.py:45
  58.6 4.2 %collective-permute-done.15.refs_10_ = f32[2,2,48,128]{3,2,1,0:T(8,128)S(1)} collective-permute-done((f32[2,2,48,128]{3,2,1,0:T(8,128)S(1)}, f32[2,2,48,128]{3,2,1,0:T(8,128)S(1)}, u32[]{:S(2)}, u32[]{:S(2)}) %collective-permute-start.15) | collective-permute-done | bytes 98336 | tf_op jit(solution)/shard_map/ppermute | solution.py:45
  64.7 1.6 %collective-permute-done.14.refs_9_ = f32[4,2,48,128]{3,2,1,0:T(8,128)S(1)} collective-permute-done((f32[4,2,48,128]{3,2,1,0:T(8,128)S(1)}, f32[4,2,48,128]{3,2,1,0:T(8,128)S(1)}, u32[]{:S(2)}, u32[]{:S(2)}) %collective-permute-start.14) | collective-permute-done | bytes 196640 | tf_op jit(solution)/shard_map/ppermute | solution.py:45
  68.5 33.2 %parareal.1 = f32[8,4,16,256]{3,2,1,0:T(8,128)} custom-call(f32[8,16]{1,0:T(8,128)} %add.50.controls, f32[4,2,80,128]{3,2,1,0:T(8,128)} %get-tuple-element.29.refs_0_, f32[4,2,80,128]{3,2,1,0:T(8,128)} %get-tuple-element.27.refs_1_, f32[4,2,64,128]{3,2,1,0:T(8,128)} %copy-done.3, f32[4,2,64,128]{3,2,1,0:T(8,128)} %copy-done.4, f32[4,2,64,128]{3,2,1,0:T(8,128)} %copy-done.1, ...), custom_call_target="tpu_custom_call" | custom-call | tf_op jit(solution)/shard_map/parareal/pallas_call | solution.py:324
  101.7 16.5 %all_to_all.5 = f32[16,2,16,256]{3,2,1,0:T(8,128)S(1)} all-to-all(f32[16,2,16,256]{3,2,1,0:T(8,128)} %bitcast.48), channel_id=1, replica_groups=mesh['tm'=8,'chip'=16,'core'=2] {'tm','core'}, dimensions={0} | all-to-all | bytes 1048576 | tf_op jit(solution)/shard_map/all_to_all | solution.py:403
  (104 shorter events, 13.3 us)
Async XLA Ops:
  2.1 10.8 %collective-permute-start.3 = (f32[82,256]{1,0:T(8,128)S(1)}, f32[82,256]{1,0:T(8,128)S(1)}, u32[]{:S(2)}, u32[]{:S(2)}) collective-permute-start(f32[82,256]{1,0:T(8,128)S(1)} %fusion.23), channel_id=1, source_target_pairs={{1,2},{2,1},{3,4},{4,3},{5,6},{6,5},{7,8},{8,7},{9,10},{10,9},{11,... | collective-permute-start | bytes 251912 | tf_op jit(solution)/shard_map/ppermute | solution.py:45
  9.3 6.4 %collective-permute-start.2 = (f32[82,256]{1,0:T(8,128)S(1)}, f32[82,256]{1,0:T(8,128)S(1)}, u32[]{:S(2)}, u32[]{:S(2)}) collective-permute-start(f32[82,256]{1,0:T(8,128)S(1)} %fusion.23), channel_id=1, source_target_pairs={{1,3},{2,0},{3,5},{4,2},{5,7},{6,4},{7,9},{8,6},{9,11},{10,8},{11,... | collective-permute-start | bytes 251912 | tf_op jit(solution)/shard_map/ppermute | solution.py:45
  12.2 3.5 %collective-permute-start = (f32[2,82,256]{2,1,0:T(8,128)S(1)}, f32[2,82,256]{2,1,0:T(8,128)S(1)}, u32[]{:S(2)}, u32[]{:S(2)}) collective-permute-start(f32[2,82,256]{2,1,0:T(8,128)S(1)} %get-tuple-element.33), channel_id=1, source_target_pairs={{0,1},{1,0},{2,3},{3,2},{4,5},{5,4},{6,7},{7,6},{8,9},{9,8},{10,11... | collective-permute-start | bytes 503816 | tf_op jit(solution)/shard_map/ppermute | solution.py:45
  12.3 6.7 %collective-permute-start.1 = (f32[2,2,82,256]{3,2,1,0:T(8,128)S(1)}, f32[2,2,82,256]{3,2,1,0:T(8,128)S(1)}, u32[]{:S(2)}, u32[]{:S(2)}) collective-permute-start(f32[2,2,82,256]{3,2,1,0:T(8,128)S(1)} %pad_maximum_fusion.2), channel_id=1, source_target_pairs={{0,1},{1,0},{2,3},{3,2},{4,5},{5,4},{6,7},{7,6},{8,9},{9,8},{10,11... | collective-permute-start | bytes 1007624 | tf_op jit(solution)/shard_map/ppermute | solution.py:45
  17.1 10.4 %collective-permute-start.5 = (f32[4,2,64,128]{3,2,1,0:T(8,128)S(1)}, f32[4,2,64,128]{3,2,1,0:T(8,128)S(1)}, u32[]{:S(2)}, u32[]{:S(2)}) collective-permute-start(f32[4,2,64,128]{3,2,1,0:T(8,128)S(1)} %fusion.10), channel_id=1, source_target_pairs={{0,2},{2,4},{3,1},{4,6},{5,3},{6,8},{7,5},{8,10},{9,7},{10,12},{11... | collective-permute-start | bytes 786440 | tf_op jit(solution)/shard_map/ppermute | solution.py:45
  20.3 10.4 %collective-permute-start.9 = (f32[4,2,64,128]{3,2,1,0:T(8,128)S(1)}, f32[4,2,64,128]{3,2,1,0:T(8,128)S(1)}, u32[]{:S(2)}, u32[]{:S(2)}) collective-permute-start(f32[4,2,64,128]{3,2,1,0:T(8,128)S(1)} %fusion.9), channel_id=1, source_target_pairs={{0,2},{2,4},{3,1},{4,6},{5,3},{6,8},{7,5},{8,10},{9,7},{10,12},{11... | collective-permute-start | bytes 786440 | tf_op jit(solution)/shard_map/ppermute | solution.py:45
  22.4 3.6 %collective-permute-start.4 = (f32[8,16]{1,0:T(8,128)S(1)}, f32[8,16]{1,0:T(8,128)S(1)}, u32[]{:S(2)}, u32[]{:S(2)}) collective-permute-start(f32[8,16]{1,0:T(8,128)S(1)} %broadcast_select_fusion), channel_id=1, source_target_pairs={{0,32},{32,0},{64,96},{96,64},{128,160},{160,128},{192,224},{224,1... | collective-permute-start | bytes 1544 | tf_op jit(solution)/shard_map/ppermute | solution.py:348
  27.5 12.7 %collective-permute-start.7 = (f32[4,2,64,128]{3,2,1,0:T(8,128)S(1)}, f32[4,2,64,128]{3,2,1,0:T(8,128)S(1)}, u32[]{:S(2)}, u32[]{:S(2)}) collective-permute-start(f32[4,2,64,128]{3,2,1,0:T(8,128)S(1)} %collective-permute-done.5.refs_2_), channel_id=1, source_target_pairs={{0,2},{2,4},{3,1},{4,6},{5,3},{6,8},{7,5},{8,10},{9,7},{10,12},{11... | collective-permute-start | bytes 786440 | tf_op jit(solution)/shard_map/ppermute | solution.py:45
  30.7 12.8 %collective-permute-start.10 = (f32[4,2,64,128]{3,2,1,0:T(8,128)S(1)}, f32[4,2,64,128]{3,2,1,0:T(8,128)S(1)}, u32[]{:S(2)}, u32[]{:S(2)}) collective-permute-start(f32[4,2,64,128]{3,2,1,0:T(8,128)S(1)} %collective-permute-done.9.refs_3_), channel_id=1, source_target_pairs={{0,2},{2,4},{3,1},{4,6},{5,3},{6,8},{7,5},{8,10},{9,7},{10,12},{11... | collective-permute-start | bytes 786440 | tf_op jit(solution)/shard_map/ppermute | solution.py:45
  35.0 5.1 %collective-permute-start.6 = (f32[8,16]{1,0:T(8,128)S(1)}, f32[8,16]{1,0:T(8,128)S(1)}, u32[]{:S(2)}, u32[]{:S(2)}) collective-permute-start(f32[8,16]{1,0:T(8,128)S(1)} %fusion.24), channel_id=1, source_target_pairs={{0,64},{32,96},{64,0},{96,32},{128,192},{160,224},{192,128},{224,1... | collective-permute-start | bytes 1544 | tf_op jit(solution)/shard_map/ppermute | solution.py:348
  38.2 8.9 %collective-permute-start.16 = (f32[4,2,64,128]{3,2,1,0:T(8,128)S(1)}, f32[4,2,64,128]{3,2,1,0:T(8,128)S(1)}, u32[]{:S(2)}, u32[]{:S(2)}) collective-permute-start(f32[4,2,64,128]{3,2,1,0:T(8,128)S(1)} %collective-permute-done.5.refs_2_), channel_id=1, source_target_pairs={{0,1},{1,0},{2,3},{3,2},{4,5},{5,4},{6,7},{7,6},{8,9},{9,8},{10,11... | collective-permute-start | bytes 786440 | tf_op jit(solution)/shard_map/ppermute | solution.py:45
  40.2 13.2 %collective-permute-start.11 = (f32[4,2,48,128]{3,2,1,0:T(8,128)S(1)}, f32[4,2,48,128]{3,2,1,0:T(8,128)S(1)}, u32[]{:S(2)}, u32[]{:S(2)}) collective-permute-start(f32[4,2,48,128]{3,2,1,0:T(8,128)S(1)} %slice.104), channel_id=1, source_target_pairs={{0,2},{2,4},{3,1},{4,6},{5,3},{6,8},{7,5},{8,10},{9,7},{10,12},{11... | collective-permute-start | bytes 589832 | tf_op jit(solution)/shard_map/ppermute | solution.py:45
  43.6 13.0 %collective-permute-start.12 = (f32[4,2,48,128]{3,2,1,0:T(8,128)S(1)}, f32[4,2,48,128]{3,2,1,0:T(8,128)S(1)}, u32[]{:S(2)}, u32[]{:S(2)}) collective-permute-start(f32[4,2,48,128]{3,2,1,0:T(8,128)S(1)} %slice.117), channel_id=1, source_target_pairs={{0,2},{2,4},{3,1},{4,6},{5,3},{6,8},{7,5},{8,10},{9,7},{10,12},{11... | collective-permute-start | bytes 589832 | tf_op jit(solution)/shard_map/ppermute | solution.py:45
  46.5 16.3 %collective-permute-start.17 = (f32[4,2,64,128]{3,2,1,0:T(8,128)S(1)}, f32[4,2,64,128]{3,2,1,0:T(8,128)S(1)}, u32[]{:S(2)}, u32[]{:S(2)}) collective-permute-start(f32[4,2,64,128]{3,2,1,0:T(8,128)S(1)} %collective-permute-done.9.refs_3_), channel_id=1, source_target_pairs={{0,1},{1,0},{2,3},{3,2},{4,5},{5,4},{6,7},{7,6},{8,9},{9,8},{10,11... | collective-permute-start | bytes 786440 | tf_op jit(solution)/shard_map/ppermute | solution.py:45
  46.7 17.5 %collective-permute-start.18 = (f32[4,2,64,128]{3,2,1,0:T(8,128)S(1)}, f32[4,2,64,128]{3,2,1,0:T(8,128)S(1)}, u32[]{:S(2)}, u32[]{:S(2)}) collective-permute-start(f32[4,2,64,128]{3,2,1,0:T(8,128)S(1)} %collective-permute-done.7.refs_4_), channel_id=1, source_target_pairs={{0,1},{1,0},{2,3},{3,2},{4,5},{5,4},{6,7},{7,6},{8,9},{9,8},{10,11... | collective-permute-start | bytes 786440 | tf_op jit(solution)/shard_map/ppermute | solution.py:45
  47.2 4.3 %collective-permute-start.8 = (f32[8,16]{1,0:T(8,128)S(1)}, f32[8,16]{1,0:T(8,128)S(1)}, u32[]{:S(2)}, u32[]{:S(2)}) collective-permute-start(f32[8,16]{1,0:T(8,128)S(1)} %add.49), channel_id=1, source_target_pairs={{0,128},{32,160},{64,192},{96,224},{128,0},{160,32},{192,64},{224,... | collective-permute-start | bytes 1544 | tf_op jit(solution)/shard_map/ppermute | solution.py:348
  51.5 11.3 %collective-permute-start.15 = (f32[2,2,48,128]{3,2,1,0:T(8,128)S(1)}, f32[2,2,48,128]{3,2,1,0:T(8,128)S(1)}, u32[]{:S(2)}, u32[]{:S(2)}) collective-permute-start(f32[2,2,48,128]{3,2,1,0:T(8,128)S(1)} %fusion.22), channel_id=1, source_target_pairs={{0,10},{2,12},{4,14},{6,144},{8,146},{10,148},{11,1},{12,150},{13,... | collective-permute-start | bytes 294920 | tf_op jit(solution)/shard_map/ppermute | solution.py:45
  53.4 11.2 %collective-permute-start.13 = (f32[4,2,48,128]{3,2,1,0:T(8,128)S(1)}, f32[4,2,48,128]{3,2,1,0:T(8,128)S(1)}, u32[]{:S(2)}, u32[]{:S(2)}) collective-permute-start(f32[4,2,48,128]{3,2,1,0:T(8,128)S(1)} %collective-permute-done.11.refs_6_), channel_id=1, source_target_pairs={{0,2},{2,4},{3,1},{4,6},{5,3},{6,8},{7,5},{8,10},{9,7},{10,12},{11... | collective-permute-start | bytes 589832 | tf_op jit(solution)/shard_map/ppermute | solution.py:45
  56.7 9.7 %collective-permute-start.14 = (f32[4,2,48,128]{3,2,1,0:T(8,128)S(1)}, f32[4,2,48,128]{3,2,1,0:T(8,128)S(1)}, u32[]{:S(2)}, u32[]{:S(2)}) collective-permute-start(f32[4,2,48,128]{3,2,1,0:T(8,128)S(1)} %collective-permute-done.12.refs_7_), channel_id=1, source_target_pairs={{0,2},{2,4},{3,1},{4,6},{5,3},{6,8},{7,5},{8,10},{9,7},{10,12},{11... | collective-permute-start | bytes 589832 | tf_op jit(solution)/shard_map/ppermute | solution.py:45
  62.9 4.1 %collective-permute-start.19 = (f32[4,2,64,128]{3,2,1,0:T(8,128)S(1)}, f32[4,2,64,128]{3,2,1,0:T(8,128)S(1)}, u32[]{:S(2)}, u32[]{:S(2)}) collective-permute-start(f32[4,2,64,128]{3,2,1,0:T(8,128)S(1)} %collective-permute-done.10.refs_5_), channel_id=1, source_target_pairs={{0,1},{1,0},{2,3},{3,2},{4,5},{5,4},{6,7},{7,6},{8,9},{9,8},{10,11... | collective-permute-start | bytes 786440 | tf_op jit(solution)/shard_map/ppermute | solution.py:45
  64.0 2.9 %collective-permute-start.20 = (f32[4,2,48,128]{3,2,1,0:T(8,128)S(1)}, f32[4,2,48,128]{3,2,1,0:T(8,128)S(1)}, u32[]{:S(2)}, u32[]{:S(2)}) collective-permute-start(f32[4,2,48,128]{3,2,1,0:T(8,128)S(1)} %collective-permute-done.11.refs_6_), channel_id=1, source_target_pairs={{0,1},{1,0},{2,3},{3,2},{4,5},{5,4},{6,7},{7,6},{8,9},{9,8},{10,11... | collective-permute-start | bytes 589832 | tf_op jit(solution)/shard_map/ppermute | solution.py:45
  64.2 2.8 %collective-permute-start.21 = (f32[4,2,48,128]{3,2,1,0:T(8,128)S(1)}, f32[4,2,48,128]{3,2,1,0:T(8,128)S(1)}, u32[]{:S(2)}, u32[]{:S(2)}) collective-permute-start(f32[4,2,48,128]{3,2,1,0:T(8,128)S(1)} %collective-permute-done.12.refs_7_), channel_id=1, source_target_pairs={{0,1},{1,0},{2,3},{3,2},{4,5},{5,4},{6,7},{7,6},{8,9},{9,8},{10,11... | collective-permute-start | bytes 589832 | tf_op jit(solution)/shard_map/ppermute | solution.py:45
  64.6 2.4 %collective-permute-start.22 = (f32[4,2,48,128]{3,2,1,0:T(8,128)S(1)}, f32[4,2,48,128]{3,2,1,0:T(8,128)S(1)}, u32[]{:S(2)}, u32[]{:S(2)}) collective-permute-start(f32[4,2,48,128]{3,2,1,0:T(8,128)S(1)} %collective-permute-done.13.refs_8_), channel_id=1, source_target_pairs={{0,1},{1,0},{2,3},{3,2},{4,5},{5,4},{6,7},{7,6},{8,9},{9,8},{10,11... | collective-permute-start | bytes 589832 | tf_op jit(solution)/shard_map/ppermute | solution.py:45
  66.3 1.4 %collective-permute-start.23 = (f32[4,2,48,128]{3,2,1,0:T(8,128)S(1)}, f32[4,2,48,128]{3,2,1,0:T(8,128)S(1)}, u32[]{:S(2)}, u32[]{:S(2)}) collective-permute-start(f32[4,2,48,128]{3,2,1,0:T(8,128)S(1)} %collective-permute-done.14.refs_9_), channel_id=1, source_target_pairs={{0,1},{1,0},{2,3},{3,2},{4,5},{5,4},{6,7},{7,6},{8,9},{9,8},{10,11... | collective-permute-start | bytes 589832 | tf_op jit(solution)/shard_map/ppermute | solution.py:45
  (24 other events, 138.6 us)
